TPU v7x, 32 devices: a whole 2x2x4 slice. The times are simulated.
32 devices in a mesh: head: 4 (over x, core), seq: 8 (over z, y).
Axes of the slice: x: 2, y: 2, z: 4, core: 2. Of those that a mesh axis runs over, the one named last changes fastest.
Arguments:
- queries: bfloat16 [12288, 4096], P('seq', 'head'), may hold values from -32 to 32
- key_rows: bfloat16 [12288, 4096], P('seq', 'head'), may hold values from -32 to 32
- value_rows: bfloat16 [12288, 4096], P('seq', 'head'), may hold values from -6 to 6
- learn_rates: bfloat16 [12288, 8], P('seq', 'head'), may hold values from 0.00025367737 to 0.0025482178
- gate_fast: float32 [8, 512, 512], P('head'), may hold values from -0.25 to 0.25
- down_fast: float32 [8, 512, 512], P('head'), may hold values from -0.25 to 0.25
- up_fast: float32 [8, 512, 512], P('head'), may hold values from -0.25 to 0.25
Outputs:
- mixed: bfloat16 [12288, 4096], P('seq', 'head')
All inputs are finite; a program needn't handle non-finite values.
Results may differ from a plain program's by a relative error of at most 0.024.
Values may be sent and summed in bfloat16 or wider, within the bound.
No kernel may reach another device: no remote copies, remote signals or barrier semaphores. Data moves between devices by JAX's collectives and lax.ppermute only.
A program may use at most 128 MiB of HBM per device.

v0:
```python
import functools
import math

import jax
import jax.numpy as jnp
from jax import lax
from jax.experimental import pallas as pl
from jax.experimental.pallas import tpu as pltpu
from jax.sharding import PartitionSpec as P


AH = 128
WINDOW = 512
EPSILON = 1e-06
F32 = jnp.float32
BF16 = jnp.bfloat16


def dot(a, b, dims=((1,), (0,))):
    return lax.dot_general(a, b, (dims, ((), ())), preferred_element_type=F32)


def unit_rows(x):
    x = x.astype(F32)
    return (x * lax.rsqrt(jnp.mean(x * x, axis=-1, keepdims=True) + EPSILON)).astype(BF16)


def sigmoid(x):
    return 0.5 * jnp.tanh(0.5 * x) + 0.5


def block_of(pos_ref, d, width):
    return pl.ds(pl.multiple_of(jnp.bitwise_xor(pos_ref[0], d) * width, width), width)


def gather_weights(pos_ref, piece_refs, w_ref):
    width = piece_refs[0].shape[-1]
    for d, piece in enumerate(piece_refs):
        for m in range(3):
            w_ref[m, :, block_of(pos_ref, d, width)] = piece[m]


def grads_kernel(parts, whole, head, pos_ref, *refs):
    n_w = 3 if whole else parts
    k_ref, v_ref, r_ref = refs[:3]
    w_in = refs[3 : 3 + n_w]
    outs = refs[3 + n_w : 3 + n_w + parts]
    w_ref, acc_ref = refs[-2:]
    step = pl.program_id(0)

    @pl.when(step == 0)
    def _():
        if whole:
            for m in range(3):
                w_ref[m] = w_in[m][0].astype(BF16)
        else:
            gather_weights(pos_ref, w_in, w_ref)
        acc_ref[...] = jnp.zeros_like(acc_ref)

    key_norm = unit_rows(k_ref[...])
    rate = jnp.transpose(jnp.broadcast_to(r_ref[head : head + 1, :].astype(F32), (8, r_ref.shape[1])))[:, :1]
    scaled = (rate * v_ref[...].astype(F32)).astype(BF16)
    gate_pre = dot(key_norm, w_ref[0])
    up_pre = dot(key_norm, w_ref[1])
    grad = dot(scaled, w_ref[2], ((1,), (1,)))
    sig = sigmoid(gate_pre)
    act = gate_pre * sig
    hidden = (act * up_pre).astype(BF16)
    gate_grad = (grad * up_pre * (sig + act * (1.0 - sig))).astype(BF16)
    up_grad = (grad * act).astype(BF16)
    over_rows = ((0,), (0,))
    acc_ref[0] += dot(key_norm, gate_grad, over_rows)
    acc_ref[1] += dot(key_norm, up_grad, over_rows)
    acc_ref[2] += dot(hidden, scaled, over_rows)

    @pl.when(step == pl.num_programs(0) - 1)
    def _():
        width = outs[0].shape[-1]
        for d, out in enumerate(outs):
            for m in range(3):
                out[m] = acc_ref[m, :, block_of(pos_ref, d, width)].astype(BF16)


def grads(pos, head, parts, keys, values, rates, weights, whole, tile=WINDOW):
    rows, hw = keys.shape[0], weights[0].shape[1]
    width = hw // parts
    row_spec = pl.BlockSpec((tile, hw), lambda i, p: (i, head))
    if whole:
        w_specs = [pl.BlockSpec((1, hw, hw), lambda i, p: (head, 0, 0))] * 3
    else:
        w_specs = [pl.BlockSpec((3, hw, width), lambda i, p: (0, 0, 0))] * parts
    return pl.pallas_call(
        functools.partial(grads_kernel, parts, whole, head),
        out_shape=[jax.ShapeDtypeStruct((3, hw, width), BF16)] * parts,
        grid_spec=pltpu.PrefetchScalarGridSpec(
            num_scalar_prefetch=1,
            grid=(rows // tile,),
            in_specs=[row_spec, row_spec, pl.BlockSpec((rates.shape[0], tile), lambda i, p: (0, i))]
            + w_specs,
            out_specs=[pl.BlockSpec((3, hw, width), lambda i, p: (0, 0, 0))] * parts,
            scratch_shapes=[pltpu.VMEM((3, hw, hw), BF16), pltpu.VMEM((3, hw, hw), F32)],
        ),
        compiler_params=pltpu.CompilerParams(dimension_semantics=("arbitrary",)),
        cost_estimate=pl.CostEstimate(
            flops=12 * rows * hw * hw,
            bytes_accessed=4 * rows * hw + 12 * hw * hw,
            transcendentals=rows * hw,
        ),
        name="grads",
    )(pos, keys, values, rates, *weights)


def tail_kernel(k_ref, v_ref, o_ref):
    o_ref[0] = k_ref[...]
    o_ref[1] = v_ref[...]


def tail_rows(keys, values, step=256):
    rows, cols = keys.shape
    first = (rows - WINDOW) // step
    spec = pl.BlockSpec((step, cols), lambda i: (first + i, 0))
    return pl.pallas_call(
        tail_kernel,
        out_shape=jax.ShapeDtypeStruct((2, WINDOW, cols), BF16),
        grid=(WINDOW // step,),
        in_specs=[spec, spec],
        out_specs=pl.BlockSpec((2, step, cols), lambda i: (0, i, 0)),
        compiler_params=pltpu.CompilerParams(dimension_semantics=("arbitrary",)),
        cost_estimate=pl.CostEstimate(flops=0, bytes_accessed=8 * WINDOW * cols, transcendentals=0),
        name="tail_rows",
    )(keys, values)


def moved_shard(weight, term):
    moved = weight + term
    target = jnp.sqrt(jnp.sum(weight * weight, axis=0, keepdims=True))
    return moved * (target / jnp.sqrt(jnp.sum(moved * moved, axis=0, keepdims=True) + EPSILON))


def renew_first_kernel(pos_ref, own_ref, far_ref, g_ref, u_ref, d_ref, w_out, bf_out):
    near = pos_ref[1] == 0
    for m, w_ref in enumerate((g_ref, u_ref, d_ref)):
        term = jnp.where(near, own_ref[m].astype(F32), far_ref[m].astype(F32))
        new = moved_shard(w_ref[0], term)
        w_out[m] = new
        bf_out[m] = new.astype(BF16)


def renew_first(pos, head, own, far, gate, up, down):
    _, hw, width = own.shape
    whole = pl.BlockSpec((3, hw, width), lambda i, p: (0, 0, 0))
    shard = pl.BlockSpec((1, hw, width), lambda i, p: (head, 0, p[0]))
    return pl.pallas_call(
        renew_first_kernel,
        out_shape=[jax.ShapeDtypeStruct(own.shape, F32), jax.ShapeDtypeStruct(own.shape, BF16)],
        grid_spec=pltpu.PrefetchScalarGridSpec(
            num_scalar_prefetch=1,
            grid=(1,),
            in_specs=[whole, whole, shard, shard, shard],
            out_specs=[whole, whole],
        ),
        cost_estimate=pl.CostEstimate(flops=18 * hw * width, bytes_accessed=40 * hw * width, transcendentals=0),
        name="renew_first",
    )(pos, own, far, gate, up, down)


def renew_second_kernel(pos_ref, *refs):
    term_refs, w_ref, bf_out = refs[:-2], refs[-2], refs[-1]
    near = pos_ref[1] == 0
    for m in range(3):
        term = term_refs[0][m].astype(F32)
        for other in term_refs[1:]:
            term += other[m].astype(F32)
        weight = w_ref[m]
        bf_out[m] = jnp.where(near, weight, moved_shard(weight, term)).astype(BF16)


def renew_second(pos, terms, weight):
    _, hw, width = weight.shape
    whole = pl.BlockSpec((3, hw, width), lambda i, p: (0, 0, 0))
    return pl.pallas_call(
        renew_second_kernel,
        out_shape=jax.ShapeDtypeStruct(weight.shape, BF16),
        grid_spec=pltpu.PrefetchScalarGridSpec(
            num_scalar_prefetch=1, grid=(1,), in_specs=[whole] * (len(terms) + 1), out_specs=whole
        ),
        cost_estimate=pl.CostEstimate(flops=24 * hw * width, bytes_accessed=40 * hw * width, transcendentals=0),
        name="renew_second",
    )(pos, *terms, weight)


def attend_tile(q, keys, values, outside, half):
    scores = [dot(q, k, ((1,), (1,))) for k in keys]
    scores = [jnp.where(out, F32(-1e30), s) if out is not None else s for s, out in zip(scores, outside)]
    row = lax.broadcasted_iota(jnp.int32, (half, half), 0)
    col = lax.broadcasted_iota(jnp.int32, (half, half), 1)
    own = col <= row
    edge = jnp.where(own, scores[2], scores[0])
    top = jnp.maximum(jnp.max(edge, axis=-1, keepdims=True), jnp.max(scores[1], axis=-1, keepdims=True))
    factor = F32(math.log2(math.e) / math.sqrt(AH))
    p_edge = jnp.exp2((edge - top) * factor)
    p_mid = jnp.exp2((scores[1] - top) * factor)
    total = jnp.sum(p_edge, axis=-1, keepdims=True) + jnp.sum(p_mid, axis=-1, keepdims=True)
    zero = jnp.zeros_like(p_edge)
    probs = [jnp.where(own, zero, p_edge), p_mid, jnp.where(own, p_edge, zero)]
    out = sum(dot(p.astype(BF16), v) for p, v in zip(probs, values))
    return (out * (1.0 / total)).astype(BF16)


def inner_kernel(q_ref, k_ref, v_ref, _, o_ref):
    half = WINDOW // 2
    for t in range(o_ref.shape[0] // half):
        keys = [k_ref[(t + j) * half : (t + j + 1) * half, :] for j in range(3)]
        values = [v_ref[(t + j) * half : (t + j + 1) * half, :] for j in range(3)]
        q = q_ref[(t + 2) * half : (t + 3) * half, :]
        o_ref[t * half : (t + 1) * half, :] = attend_tile(q, keys, values, (None, None, None), half)


def inner_attention(queries, keys, values, first, count, after):
    rows = queries.shape[0]
    strip = pl.BlockSpec((rows, AH), lambda a: (0, first + a))
    return pl.pallas_call(
        inner_kernel,
        out_shape=jax.ShapeDtypeStruct((rows - WINDOW, count * AH), BF16),
        grid=(count,),
        in_specs=[strip] * 3 + [pl.BlockSpec(memory_space=pl.ANY)],
        out_specs=pl.BlockSpec((rows - WINDOW, AH), lambda a: (0, a)),
        compiler_params=pltpu.CompilerParams(dimension_semantics=("arbitrary",)),
        cost_estimate=pl.CostEstimate(
            flops=count * rows * WINDOW * AH * 6,
            bytes_accessed=count * rows * AH * 10,
            transcendentals=count * rows * WINDOW,
        ),
        name="inner_attention",
    )(queries, keys, values, after)


def edge_kernel(side, pos_ref, q_ref, k_ref, v_ref, h_ref, *refs):
    o_ref = refs[-1]
    half = WINDOW // 2
    active = pos_ref[1] == side

    @pl.when(active)
    def _():
        first = pos_ref[2] == 0
        keys = [h_ref[0, :half], h_ref[0, half:], k_ref[:half, :], k_ref[half:, :]]
        values = [h_ref[1, :half], h_ref[1, half:], v_ref[:half, :], v_ref[half:, :]]
        for t in range(2):
            outside = [first if j + t < 2 else None for j in range(3)]
            o_ref[t * half : (t + 1) * half, :] = attend_tile(
                q_ref[t * half : (t + 1) * half, :], keys[t : t + 3], values[t : t + 3], outside, half
            )

    @pl.when(jnp.logical_not(active))
    def _():
        o_ref[...] = refs[0][...] if len(refs) > 1 else jnp.zeros_like(o_ref)


def edge_attention(pos, queries, keys, values, halo, before, side):
    count = queries.shape[1] // AH
    strip = pl.BlockSpec((WINDOW, AH), lambda a, p: (0, jnp.where(p[1] == side, a, 0)))
    return pl.pallas_call(
        functools.partial(edge_kernel, side),
        out_shape=jax.ShapeDtypeStruct((WINDOW, count * AH), BF16),
        grid_spec=pltpu.PrefetchScalarGridSpec(
            num_scalar_prefetch=1,
            grid=(count,),
            in_specs=[strip, strip, strip]
            + [pl.BlockSpec((2, WINDOW, AH), lambda a, p: (0, 0, jnp.where(p[1] == side, a, 0)))]
            + [pl.BlockSpec((WINDOW, AH), lambda a, p: (0, 0))] * len(before),
            out_specs=strip,
        ),
        input_output_aliases={5: 0} if before else {},
        compiler_params=pltpu.CompilerParams(dimension_semantics=("arbitrary",)),
        cost_estimate=pl.CostEstimate(
            flops=count * WINDOW * WINDOW * AH * 6,
            bytes_accessed=count * WINDOW * AH * 18,
            transcendentals=count * WINDOW * WINDOW,
        ),
        name="edge_attention",
    )(pos, queries, keys, values, halo, *before)


def apply_kernel(parts, pos_ref, *refs):
    q_ref, edge_ref, inner_ref = refs[:3]
    pieces = refs[3 : 3 + parts]
    o_ref, w_ref = refs[-2:]
    step = pl.program_id(0)

    @pl.when(step == 0)
    def _():
        gather_weights(pos_ref, pieces, w_ref)

    query_norm = unit_rows(q_ref[...])
    gate_pre = dot(query_norm, w_ref[0])
    up_pre = dot(query_norm, w_ref[1])
    hidden = (gate_pre * sigmoid(gate_pre) * up_pre).astype(BF16)
    fast = dot(hidden, w_ref[2]).astype(BF16).astype(F32)

    @pl.when(step == 0)
    def _():
        o_ref[...] = (fast + edge_ref[...].astype(F32)).astype(BF16)

    @pl.when(step > 0)
    def _():
        o_ref[...] = (fast + inner_ref[...].astype(F32)).astype(BF16)


def apply_fast(pos, head, queries, edge, inner, pieces, before):
    rows, cols = queries.shape
    parts = len(pieces)
    _, hw, width = pieces[0].shape
    in_specs = [
        pl.BlockSpec((WINDOW, hw), lambda i, p: (i, head)),
        pl.BlockSpec((WINDOW, hw), lambda i, p: (0, head)),
        pl.BlockSpec((WINDOW, hw), lambda i, p: (jnp.maximum(i - 1, 0), 0)),
    ] + [pl.BlockSpec((3, hw, width), lambda i, p: (0, 0, 0))] * parts
    operands = [pos, queries, edge, inner, *pieces]
    aliases = {}
    if before is not None:
        in_specs.append(pl.BlockSpec(memory_space=pl.ANY))
        aliases = {len(operands): 0}
        operands.append(before)
    return pl.pallas_call(
        functools.partial(apply_kernel, parts),
        out_shape=jax.ShapeDtypeStruct((rows, cols), BF16),
        grid_spec=pltpu.PrefetchScalarGridSpec(
            num_scalar_prefetch=1,
            grid=(rows // WINDOW,),
            in_specs=in_specs,
            out_specs=pl.BlockSpec((WINDOW, hw), lambda i, p: (i, head)),
            scratch_shapes=[pltpu.VMEM((3, hw, hw), BF16)],
        ),
        input_output_aliases=aliases,
        compiler_params=pltpu.CompilerParams(dimension_semantics=("arbitrary",)),
        cost_estimate=pl.CostEstimate(
            flops=6 * rows * hw * hw, bytes_accessed=8 * rows * hw + 6 * hw * hw, transcendentals=rows * hw
        ),
        name="apply_fast",
    )(*operands)


def hop(x, route):
    return lax.ppermute(x, "seq", route)


def spread(xs, low, high):
    return [hop(x, [(i, i ^ d) for i in range(low, high)]) for d, x in enumerate(xs) if d]


def fast_device(queries, key_rows, value_rows, learn_rates, gate_fast, down_fast, up_fast):
    heads, hw = gate_fast.shape[:2]
    seq_count = lax.axis_size("seq")
    parts = seq_count // 2
    seq_index = lax.axis_index("seq").astype(jnp.int32)
    pos = jnp.stack([seq_index % parts, seq_index // parts, seq_index])
    early = [(i, i + 1) for i in range(parts - 1, seq_count - 1)]
    late = [(i, i + 1) for i in range(parts - 1)]
    across = [(i, i + parts) for i in range(parts)]
    per_head = hw // AH
    rates = learn_rates.T
    first_w = (gate_fast, up_fast, down_fast)
    span = range(heads)

    tail = tail_rows(key_rows, value_rows)
    halo_a = hop(tail, early)
    terms = [grads(pos, h, parts, key_rows, value_rows, rates, first_w, True) for h in span]
    shards, w1, far, inner = [], [], [], []
    for h in span:
        got = spread(terms[h], 0, parts)
        own = terms[h][0].astype(F32)
        for g in got:
            own = own + g.astype(F32)
        own = own.astype(BF16)
        far.append(hop(own, across))
        inner.append(inner_attention(queries, key_rows, value_rows, h * per_head, per_head, own))
        shard, shard_bf = renew_first(pos, h, own, far[h], *first_w)
        shards.append(shard)
        w1.append([shard_bf] + spread([shard_bf] * parts, parts, seq_count))
    edge = edge_attention(pos, queries, key_rows, value_rows, halo_a, (), 1)
    tail, _ = lax.optimization_barrier((tail, far[-1]))
    halo_b = hop(tail, late)
    w2 = []
    for h in span:
        term = grads(pos, h, parts, key_rows, value_rows, rates, w1[h], False)
        got = [term[0]] + spread(term, parts, seq_count)
        shard_bf = renew_second(pos, got, shards[h])
        w2.append([shard_bf] + spread([shard_bf] * parts, 0, seq_count))
    edge = edge_attention(pos, queries, key_rows, value_rows, halo_b, (edge,), 0)
    out = None
    for h in span:
        out = apply_fast(pos, h, queries, edge, inner[h], w2[h], out)
    return out


def shifted(block, axis, distance):
    devices = range(lax.axis_size(axis))
    route = [(i - distance, i) for i in devices if i - distance in devices]
    return lax.ppermute(block, axis, route)


def norm_rows(values_in, heads_local, head_width):
    as_float = values_in.reshape(values_in.shape[0], heads_local, head_width).astype(jnp.float32)
    return (
        as_float / jnp.sqrt(jnp.mean(as_float * as_float, axis=-1, keepdims=True) + EPSILON)
    ).astype(jnp.bfloat16)


def fast_terms(fast_bf, key_norm, value_heads, rate_rows):
    gate_w, down_w, up_w = fast_bf
    gate_pre = jnp.einsum("nhd,hdf->nhf", key_norm, gate_w, preferred_element_type=jnp.float32)
    up_pre = jnp.einsum("nhd,hdf->nhf", key_norm, up_w, preferred_element_type=jnp.float32)
    sigmoid_gate = jax.nn.sigmoid(gate_pre)
    gate_act = gate_pre * sigmoid_gate
    hidden = (gate_act * up_pre).astype(jnp.bfloat16)
    scaled_val = (
        rate_rows.astype(jnp.float32)[:, :, None] * value_heads.astype(jnp.float32)
    ).astype(jnp.bfloat16)
    hidden_grad = -jnp.einsum(
        "nhe,hfe->nhf", scaled_val, down_w, preferred_element_type=jnp.float32
    )
    gate_grad = (
        hidden_grad * up_pre * sigmoid_gate * (1.0 + gate_pre * (1.0 - sigmoid_gate))
    ).astype(jnp.bfloat16)
    up_grad = (hidden_grad * gate_act).astype(jnp.bfloat16)
    gate_term = jnp.einsum("nhd,nhf->hdf", key_norm, gate_grad, preferred_element_type=jnp.float32)
    down_term = -jnp.einsum("nhf,nhe->hfe", hidden, scaled_val, preferred_element_type=jnp.float32)
    up_term = jnp.einsum("nhd,nhf->hdf", key_norm, up_grad, preferred_element_type=jnp.float32)
    return (gate_term, down_term, up_term)


def rescale(weight, moved):
    target_norm = jnp.sqrt(jnp.sum(weight * weight, axis=-2, keepdims=True))
    return moved * target_norm / jnp.sqrt(jnp.sum(moved * moved, axis=-2, keepdims=True) + EPSILON)


def general_apply(fast_bf, query_norm):
    gate_w, down_w, up_w = fast_bf
    gate_pre = jnp.einsum("nhd,hdf->nhf", query_norm, gate_w, preferred_element_type=jnp.float32)
    up_pre = jnp.einsum("nhd,hdf->nhf", query_norm, up_w, preferred_element_type=jnp.float32)
    hidden = (gate_pre * jax.nn.sigmoid(gate_pre) * up_pre).astype(jnp.bfloat16)
    return jnp.einsum("nhf,hfe->nhe", hidden, down_w, preferred_element_type=jnp.float32).astype(
        jnp.bfloat16
    )


def renew(fast_f32, grad_terms):
    grad_sums = lax.psum((grad_terms[0], grad_terms[1], grad_terms[2]), "seq")
    renewed = tuple(
        (rescale(weight, weight - summed) for weight, summed in zip(fast_f32, grad_sums))
    )
    renewed_bf = tuple((weight.astype(jnp.bfloat16) for weight in renewed))
    return (renewed, renewed_bf)


def general_device(queries, key_rows, value_rows, learn_rates, gate_fast, down_fast, up_fast):
    heads_local = gate_fast.shape[0]
    head_width = gate_fast.shape[1]
    seq_count = lax.axis_size("seq")
    seq_index = lax.axis_index("seq")
    rows_here = queries.shape[0]
    width_here = queries.shape[1]
    fast_f32 = (gate_fast, down_fast, up_fast)
    first_bf = tuple((weight.astype(jnp.bfloat16) for weight in fast_f32))
    own_group = (seq_index >= seq_count // 2).astype(jnp.int32)
    query_norm = norm_rows(queries, heads_local, head_width)
    key_norm = norm_rows(key_rows, heads_local, head_width)
    value_heads = value_rows.reshape(rows_here, heads_local, head_width)
    fast_bf = first_bf
    kept = []
    for group in range(2):
        group_rates = jnp.where(own_group == group, learn_rates, jnp.zeros_like(learn_rates))
        grad_terms = fast_terms(fast_bf, key_norm, value_heads, group_rates)
        fast_f32, fast_bf = renew(fast_f32, grad_terms)
        kept.append(fast_bf)
    chosen = tuple(
        (jnp.where(own_group == 0, early, later) for early, later in zip(kept[0], kept[1]))
    )
    fast_out = general_apply(chosen, query_norm).reshape(rows_here, width_here)
    attn_heads = width_here // AH
    score_scale = 1.0 / math.sqrt(AH)
    prev_keys, prev_values = shifted(
        (key_rows[rows_here - WINDOW :], value_rows[rows_here - WINDOW :]), "seq", 1
    )
    wide_keys = jnp.concatenate([prev_keys, key_rows], axis=0)
    wide_values = jnp.concatenate([prev_values, value_rows], axis=0)
    query_offset = jnp.arange(WINDOW, dtype=jnp.int32)[:, None]
    key_offset = jnp.arange(2 * WINDOW, dtype=jnp.int32)[None, :]
    block_outs = []
    for block in range(rows_here // WINDOW):
        lower = block * WINDOW
        start = seq_index * rows_here + lower
        query_block = queries[lower : lower + WINDOW].reshape(WINDOW, attn_heads, AH)
        key_block = wide_keys[lower : lower + 2 * WINDOW].reshape(2 * WINDOW, attn_heads, AH)
        value_block = wide_values[lower : lower + 2 * WINDOW].reshape(2 * WINDOW, attn_heads, AH)
        scores = (
            jnp.einsum("qhd,khd->hqk", query_block, key_block, preferred_element_type=jnp.float32)
            * score_scale
        )
        query_pos = start + query_offset
        key_pos = start - WINDOW + key_offset
        allowed = (key_pos <= query_pos) & (key_pos > query_pos - WINDOW) & (key_pos >= 0)
        scores = jnp.where(allowed[None], scores, jnp.float32(-1e30))
        top_score = jnp.max(scores, axis=-1, keepdims=True)
        expo = jnp.exp(scores - top_score)
        attend = (expo / jnp.sum(expo, axis=-1, keepdims=True)).astype(jnp.bfloat16)
        block_outs.append(
            jnp.einsum(
                "hqk,khd->qhd", attend, value_block, preferred_element_type=jnp.float32
            ).reshape(WINDOW, width_here)
        )
    attended = jnp.concatenate(block_outs, axis=0)
    return (fast_out.astype(jnp.float32) + attended).astype(jnp.bfloat16)


def solution(mesh):
    parts = mesh.shape["seq"] // 2

    def fits(args):
        width = args[4].shape[1] // parts
        return parts & (parts - 1) == 0 and width % AH == 0 and args[0].shape[0] >= 2 * WINDOW

    def on_device(*args):
        if fits(args):
            return fast_device(*args)
        return general_device(*args)

    return jax.shard_map(
        on_device,
        mesh=mesh,
        in_specs=(
            P("seq", "head"),
            P("seq", "head"),
            P("seq", "head"),
            P("seq", "head"),
            P("head", None, None),
            P("head", None, None),
            P("head", None, None),
        ),
        out_specs=P("seq", "head"),
        check_vma=False,
    )
```

profile of v0, /device:TPU:26, one launch (start us, length us, event | category | flops | bytes accessed | tf_op | source)
XLA Modules:
  0.0 258.3 jit_solution(15957230223285425192)
XLA Ops:
  0.7 11.8 %grads.6 = (bf16[3,512,128]{2,1,0:T(8,128)(2,1)}, bf16[3,512,128]{2,1,0:T(8,128)(2,1)}, bf16[3,512,128]{2,1,0:T(8,128)(2,1)}, bf16[3,512,128]{2,1,0:T(8,128)(2,1)}) custom-call(s32[3]{0:T(128)} %pad_add_fusion.pos_ref, bf16[1536,1024]{1,0:T(8,128)(2,1)} %refs_0_.9, bf16[1536,1024]{1,0:T(8,128)(2,1)} %refs_1_.7, bf16[2,1536]{1,0:T(2,128)(2,1)} %bitcast.4, ...), custom_call_target="tpu_custom_call" | custom-call | flops 4831838208 | bytes 6291456 | tf_op jit(solution)/shard_map/grads/pallas_call | solution.py:92
  14.7 11.8 %grads.4 = (bf16[3,512,128]{2,1,0:T(8,128)(2,1)}, bf16[3,512,128]{2,1,0:T(8,128)(2,1)}, bf16[3,512,128]{2,1,0:T(8,128)(2,1)}, bf16[3,512,128]{2,1,0:T(8,128)(2,1)}) custom-call(s32[3]{0:T(128)} %pad_add_fusion.pos_ref, bf16[1536,1024]{1,0:T(8,128)(2,1)} %refs_0_.9, bf16[1536,1024]{1,0:T(8,128)(2,1)} %refs_1_.7, bf16[2,1536]{1,0:T(2,128)(2,1)} %bitcast.5, ...), custom_call_target="tpu_custom_call" | custom-call | flops 4831838208 | bytes 6291456 | tf_op jit(solution)/shard_map/grads/pallas_call | solution.py:92
  31.8 20.5 %collective-permute-done.18.far_ref = bf16[3,512,128]{2,1,0:T(8,128)(2,1)S(1)} collective-permute-done((bf16[3,512,128]{2,1,0:T(8,128)(2,1)S(1)}, bf16[3,512,128]{2,1,0:T(8,128)(2,1)S(1)}, u32[]{:S(2)}, u32[]{:S(2)}) %collective-permute-start.18) | collective-permute-done | bytes 393248 | tf_op jit(solution)/shard_map/ppermute | solution.py:344
  53.0 3.4 %renew_first.3 = (f32[3,512,128]{2,1,0:T(8,128)}, bf16[3,512,128]{2,1,0:T(8,128)(2,1)}) custom-call(s32[3]{0:T(128)} %pad_add_fusion.pos_ref, bf16[3,512,128]{2,1,0:T(8,128)(2,1)} %copy-done, bf16[3,512,128]{2,1,0:T(8,128)(2,1)} %copy-done.7, f32[2,512,512]{2,1,0:T(8,128)} %g_ref.3, f32[2,512,512]{2,1,0:T(8,128)} %u_ref.3, f32[2,512,512]{2,1,0:T(8,128)} %d_ref.3), custom_call_target="tpu_custom_call" | custom-call | flops 1179648 | bytes 2621440 | tf_op jit(solution)/shard_map/renew_first/pallas_call | solution.py:153
  56.4 3.4 %collective-permute-start.19 = (bf16[3,512,128]{2,1,0:T(8,128)(2,1)}, bf16[3,512,128]{2,1,0:T(8,128)(2,1)S(1)}, u32[]{:S(2)}, u32[]{:S(2)}) collective-permute-start(bf16[3,512,128]{2,1,0:T(8,128)(2,1)} %get-tuple-element.41.refs_3_), channel_id=1, source_target_pairs={{4,5},{5,4},{6,7},{7,6},{12,13},{13,12},{14,15},{15,14},{20,21},{2... | collective-permute-start | bytes 1179656 | tf_op jit(solution)/shard_map/ppermute | solution.py:344
  59.8 17.2 %collective-permute-start.20 = (bf16[3,512,128]{2,1,0:T(8,128)(2,1)}, bf16[3,512,128]{2,1,0:T(8,128)(2,1)}, u32[]{:S(2)}, u32[]{:S(2)}) collective-permute-start(bf16[3,512,128]{2,1,0:T(8,128)(2,1)} %get-tuple-element.41.refs_3_), channel_id=1, source_target_pairs={{4,6},{5,7},{6,4},{7,5},{12,14},{13,15},{14,12},{15,13},{20,22},{2... | collective-permute-start | bytes 1179656 | tf_op jit(solution)/shard_map/ppermute | solution.py:344
  87.0 3.4 %renew_first.2 = (f32[3,512,128]{2,1,0:T(8,128)}, bf16[3,512,128]{2,1,0:T(8,128)(2,1)}) custom-call(s32[3]{0:T(128)} %pad_add_fusion.pos_ref, bf16[3,512,128]{2,1,0:T(8,128)(2,1)} %copy-done.1, bf16[3,512,128]{2,1,0:T(8,128)(2,1)} %copy-done.6, f32[2,512,512]{2,1,0:T(8,128)} %g_ref.3, f32[2,512,512]{2,1,0:T(8,128)} %u_ref.3, f32[2,512,512]{2,1,0:T(8,128)} %d_ref.3), custom_call_target="tpu_custom_call" | custom-call | flops 1179648 | bytes 2621440 | tf_op jit(solution)/shard_map/renew_first/pallas_call | solution.py:153
  92.3 52.5 %collective-permute-start.7 = (bf16[3,512,128]{2,1,0:T(8,128)(2,1)}, bf16[3,512,128]{2,1,0:T(8,128)(2,1)S(1)}, u32[]{:S(2)}, u32[]{:S(2)}) collective-permute-start(bf16[3,512,128]{2,1,0:T(8,128)(2,1)} %get-tuple-element.31.refs_3_), channel_id=1, source_target_pairs={{4,6},{5,7},{6,4},{7,5},{12,14},{13,15},{14,12},{15,13},{20,22},{2... | collective-permute-start | bytes 1179656 | tf_op jit(solution)/shard_map/ppermute | solution.py:344
  144.8 3.4 %collective-permute-start.8 = (bf16[3,512,128]{2,1,0:T(8,128)(2,1)}, bf16[3,512,128]{2,1,0:T(8,128)(2,1)}, u32[]{:S(2)}, u32[]{:S(2)}) collective-permute-start(bf16[3,512,128]{2,1,0:T(8,128)(2,1)} %get-tuple-element.31.refs_3_), channel_id=1, source_target_pairs={{4,7},{5,6},{6,5},{7,4},{12,15},{13,14},{14,13},{15,12},{20,23},{2... | collective-permute-start | bytes 1179656 | tf_op jit(solution)/shard_map/ppermute | solution.py:344
  148.1 11.4 %grads.7 = (bf16[3,512,128]{2,1,0:T(8,128)(2,1)}, bf16[3,512,128]{2,1,0:T(8,128)(2,1)}, bf16[3,512,128]{2,1,0:T(8,128)(2,1)}, bf16[3,512,128]{2,1,0:T(8,128)(2,1)}) custom-call(s32[3]{0:T(128)} %pad_add_fusion.pos_ref, bf16[1536,1024]{1,0:T(8,128)(2,1)} %refs_0_.9, bf16[1536,1024]{1,0:T(8,128)(2,1)} %refs_1_.7, bf16[2,1536]{1,0:T(2,128)(2,1)} %bitcast.6, ...), custom_call_target="tpu_custom_call" | custom-call | flops 4831838208 | bytes 6291456 | tf_op jit(solution)/shard_map/grads/pallas_call | solution.py:92
  162.8 3.4 %collective-permute-start.23 = (bf16[3,512,128]{2,1,0:T(8,128)(2,1)}, bf16[3,512,128]{2,1,0:T(8,128)(2,1)S(1)}, u32[]{:S(2)}, u32[]{:S(2)}) collective-permute-start(bf16[3,512,128]{2,1,0:T(8,128)(2,1)} %get-tuple-element.44), channel_id=1, source_target_pairs={{4,6},{5,7},{6,4},{7,5},{12,14},{13,15},{14,12},{15,13},{20,22},{2... | collective-permute-start | bytes 1179656 | tf_op jit(solution)/shard_map/ppermute | solution.py:344
  166.2 3.6 %collective-permute-start.24 = (bf16[3,512,128]{2,1,0:T(8,128)(2,1)}, bf16[3,512,128]{2,1,0:T(8,128)(2,1)S(1)}, u32[]{:S(2)}, u32[]{:S(2)}) collective-permute-start(bf16[3,512,128]{2,1,0:T(8,128)(2,1)} %get-tuple-element.45), channel_id=1, source_target_pairs={{4,7},{5,6},{6,5},{7,4},{12,15},{13,14},{14,13},{15,12},{20,23},{2... | collective-permute-start | bytes 1179656 | tf_op jit(solution)/shard_map/ppermute | solution.py:344
  169.8 11.4 %grads.5 = (bf16[3,512,128]{2,1,0:T(8,128)(2,1)}, bf16[3,512,128]{2,1,0:T(8,128)(2,1)}, bf16[3,512,128]{2,1,0:T(8,128)(2,1)}, bf16[3,512,128]{2,1,0:T(8,128)(2,1)}) custom-call(s32[3]{0:T(128)} %pad_add_fusion.pos_ref, bf16[1536,1024]{1,0:T(8,128)(2,1)} %refs_0_.9, bf16[1536,1024]{1,0:T(8,128)(2,1)} %refs_1_.7, bf16[2,1536]{1,0:T(2,128)(2,1)} %bitcast.7, ...), custom_call_target="tpu_custom_call" | custom-call | flops 4831838208 | bytes 6291456 | tf_op jit(solution)/shard_map/grads/pallas_call | solution.py:92
  181.2 3.9 %collective-permute-start.10 = (bf16[3,512,128]{2,1,0:T(8,128)(2,1)}, bf16[3,512,128]{2,1,0:T(8,128)(2,1)}, u32[]{:S(2)}, u32[]{:S(2)}) collective-permute-start(bf16[3,512,128]{2,1,0:T(8,128)(2,1)} %get-tuple-element.34), channel_id=1, source_target_pairs={{4,6},{5,7},{6,4},{7,5},{12,14},{13,15},{14,12},{15,13},{20,22},{2... | collective-permute-start | bytes 1179656 | tf_op jit(solution)/shard_map/ppermute | solution.py:344
  187.1 3.4 %collective-permute-start.9 = (bf16[3,512,128]{2,1,0:T(8,128)(2,1)}, bf16[3,512,128]{2,1,0:T(8,128)(2,1)}, u32[]{:S(2)}, u32[]{:S(2)}) collective-permute-start(bf16[3,512,128]{2,1,0:T(8,128)(2,1)} %get-tuple-element.33), channel_id=1, source_target_pairs={{4,5},{5,4},{6,7},{7,6},{12,13},{13,12},{14,15},{15,14},{20,21},{2... | collective-permute-start | bytes 1179656 | tf_op jit(solution)/shard_map/ppermute | solution.py:344
  190.5 3.5 %renew_second.3.refs_3_ = bf16[3,512,128]{2,1,0:T(8,128)(2,1)} custom-call(s32[3]{0:T(128)} %pad_add_fusion.pos_ref, bf16[3,512,128]{2,1,0:T(8,128)(2,1)} %get-tuple-element.42.refs_0_, bf16[3,512,128]{2,1,0:T(8,128)(2,1)} %copy-done.8, bf16[3,512,128]{2,1,0:T(8,128)(2,1)} %copy-done.10, bf16[3,512,128]{2,1,0:T(8,128)(2,1)} %copy-done.12, ...), custom_call_target="tpu_custom_call" | custom-call | flops 1572864 | bytes 2621440 | tf_op jit(solution)/shard_map/renew_second/pallas_call | solution.py:181
  194.9 8.9 %inner_attention.3.refs_2_ = bf16[1024,512]{1,0:T(8,128)(2,1)} custom-call(bf16[1536,1024]{1,0:T(8,128)(2,1)} %refs_0_.11, bf16[1536,1024]{1,0:T(8,128)(2,1)} %refs_0_.9, bf16[1536,1024]{1,0:T(8,128)(2,1)} %refs_1_.7, bf16[3,512,128]{2,1,0:T(8,128)(2,1)} %copy-done), custom_call_target="tpu_custom_call" | custom-call | flops 2415919104 | bytes 7864320 | tf_op jit(solution)/shard_map/inner_attention/pallas_call | solution.py:222
  207.6 4.9 %collective-permute-start.27 = (bf16[3,512,128]{2,1,0:T(8,128)(2,1)S(1)}, bf16[3,512,128]{2,1,0:T(8,128)(2,1)}, u32[]{:S(2)}, u32[]{:S(2)}) collective-permute-start(bf16[3,512,128]{2,1,0:T(8,128)(2,1)S(1)} %copy-done.3), channel_id=1, source_target_pairs={{0,3},{1,2},{2,1},{3,0},{4,7},{5,6},{6,5},{7,4},{8,11},{9,10},{10,... | collective-permute-start | bytes 1179656 | tf_op jit(solution)/shard_map/ppermute | solution.py:344
  212.5 9.0 %inner_attention.2.refs_2_ = bf16[1024,512]{1,0:T(8,128)(2,1)} custom-call(bf16[1536,1024]{1,0:T(8,128)(2,1)} %refs_0_.11, bf16[1536,1024]{1,0:T(8,128)(2,1)} %refs_0_.9, bf16[1536,1024]{1,0:T(8,128)(2,1)} %refs_1_.7, bf16[3,512,128]{2,1,0:T(8,128)(2,1)} %copy-done.1), custom_call_target="tpu_custom_call" | custom-call | flops 2415919104 | bytes 7864320 | tf_op jit(solution)/shard_map/inner_attention/pallas_call | solution.py:222
  221.5 3.5 %renew_second.2.refs_3_ = bf16[3,512,128]{2,1,0:T(8,128)(2,1)} custom-call(s32[3]{0:T(128)} %pad_add_fusion.pos_ref, bf16[3,512,128]{2,1,0:T(8,128)(2,1)} %get-tuple-element.32.refs_0_, bf16[3,512,128]{2,1,0:T(8,128)(2,1)} %collective-permute-done.9.refs_1_, bf16[3,512,128]{2,1,0:T(8,128)(2,1)} %collective-permute-done.10.refs_2_, ...), custom_call_target="tpu_custom_call" | custom-call | flops 1572864 | bytes 2621440 | tf_op jit(solution)/shard_map/renew_second/pallas_call | solution.py:181
  228.5 11.1 %edge_attention.2.refs_0_ = bf16[512,1024]{1,0:T(8,128)(2,1)} custom-call(s32[3]{0:T(128)} %pad_add_fusion.pos_ref, bf16[1536,1024]{1,0:T(8,128)(2,1)} %refs_0_.11, bf16[1536,1024]{1,0:T(8,128)(2,1)} %refs_0_.9, bf16[1536,1024]{1,0:T(8,128)(2,1)} %refs_1_.7, bf16[2,512,1024]{2,1,0:T(8,128)(2,1)} %copy-done.2), custom_call_target="tpu_custom_call" | custom-call | flops 1610612736 | bytes 9437184 | tf_op jit(solution)/shard_map/edge_attention/pallas_call | solution.py:262
  239.7 3.2 %edge_attention.3.refs_1_ = bf16[512,1024]{1,0:T(8,128)(2,1)} custom-call(s32[3]{0:T(128)} %pad_add_fusion.pos_ref, bf16[1536,1024]{1,0:T(8,128)(2,1)} %refs_0_.11, bf16[1536,1024]{1,0:T(8,128)(2,1)} %refs_0_.9, bf16[1536,1024]{1,0:T(8,128)(2,1)} %refs_1_.7, bf16[2,512,1024]{2,1,0:T(8,128)(2,1)} %collective-permute-done.4.h_ref, ...), custom_call_target="tpu_custom_call", output_to_operand_aliasing={{}: (5, {})} | custom-call | flops 1610612736 | bytes 9437184 | tf_op jit(solution)/shard_map/edge_attention/pallas_call | solution.py:262
  243.6 7.3 %apply_fast.2.refs_7_ = bf16[1536,1024]{1,0:T(8,128)(2,1)} custom-call(s32[3]{0:T(128)} %pad_add_fusion.pos_ref, bf16[1536,1024]{1,0:T(8,128)(2,1)} %refs_0_.11, bf16[512,1024]{1,0:T(8,128)(2,1)} %edge_attention.3.refs_1_, bf16[1024,512]{1,0:T(8,128)(2,1)} %inner_attention.3.refs_2_, bf16[3,512,128]{2,1,0:T(8,128)(2,1)} %renew_second.3.refs_3_, ...), custom_call_target="tpu_custom_call" | custom-call | flops 2415919104 | bytes 7864320 | tf_op jit(solution)/shard_map/apply_fast/pallas_call | solution.py:324
  250.9 7.3 %apply_fast.3 = bf16[1536,1024]{1,0:T(8,128)(2,1)} custom-call(s32[3]{0:T(128)} %pad_add_fusion.pos_ref, bf16[1536,1024]{1,0:T(8,128)(2,1)} %refs_0_.11, bf16[512,1024]{1,0:T(8,128)(2,1)} %edge_attention.3.refs_1_, bf16[1024,512]{1,0:T(8,128)(2,1)} %inner_attention.2.refs_2_, ...), custom_call_target="tpu_custom_call", output_to_operand_aliasing={{}: (8, {})} | custom-call | flops 2415919104 | bytes 7864320 | tf_op jit(solution)/shard_map/apply_fast/pallas_call | solution.py:324
  (82 shorter events, 34.7 us)
Async XLA Ops:
  12.5 15.5 %collective-permute-start.15 = (bf16[3,512,128]{2,1,0:T(8,128)(2,1)}, bf16[3,512,128]{2,1,0:T(8,128)(2,1)S(1)}, u32[]{:S(2)}, u32[]{:S(2)}) collective-permute-start(bf16[3,512,128]{2,1,0:T(8,128)(2,1)} %get-tuple-element.38), channel_id=1, source_target_pairs={{0,1},{1,0},{2,3},{3,2},{8,9},{9,8},{10,11},{11,10},{16,17},{17,16... | collective-permute-start | bytes 1179656 | tf_op jit(solution)/shard_map/ppermute | solution.py:344
  13.1 15.5 %collective-permute-start.16 = (bf16[3,512,128]{2,1,0:T(8,128)(2,1)}, bf16[3,512,128]{2,1,0:T(8,128)(2,1)S(1)}, u32[]{:S(2)}, u32[]{:S(2)}) collective-permute-start(bf16[3,512,128]{2,1,0:T(8,128)(2,1)} %get-tuple-element.39), channel_id=1, source_target_pairs={{0,2},{1,3},{2,0},{3,1},{8,10},{9,11},{10,8},{11,9},{16,18},{17,19... | collective-permute-start | bytes 1179656 | tf_op jit(solution)/shard_map/ppermute | solution.py:344
  13.8 14.8 %collective-permute-start.17 = (bf16[3,512,128]{2,1,0:T(8,128)(2,1)}, bf16[3,512,128]{2,1,0:T(8,128)(2,1)S(1)}, u32[]{:S(2)}, u32[]{:S(2)}) collective-permute-start(bf16[3,512,128]{2,1,0:T(8,128)(2,1)} %get-tuple-element.40), channel_id=1, source_target_pairs={{0,3},{1,2},{2,1},{3,0},{8,11},{9,10},{10,9},{11,8},{16,19},{17,18... | collective-permute-start | bytes 1179656 | tf_op jit(solution)/shard_map/ppermute | solution.py:344
  28.9 23.3 %collective-permute-start.18 = (bf16[3,512,128]{2,1,0:T(8,128)(2,1)S(1)}, bf16[3,512,128]{2,1,0:T(8,128)(2,1)S(1)}, u32[]{:S(2)}, u32[]{:S(2)}) collective-permute-start(bf16[3,512,128]{2,1,0:T(8,128)(2,1)S(1)} %add_convert_fusion._.own_ref), channel_id=1, source_target_pairs={{0,4},{1,5},{2,6},{3,7},{8,12},{9,13},{10,14},{11,15},{16,20},{17,... | collective-permute-start | bytes 1179656 | tf_op jit(solution)/shard_map/ppermute | solution.py:344
  30.5 54.5 %collective-permute-start.3 = (bf16[3,512,128]{2,1,0:T(8,128)(2,1)S(1)}, bf16[3,512,128]{2,1,0:T(8,128)(2,1)S(1)}, u32[]{:S(2)}, u32[]{:S(2)}) collective-permute-start(bf16[3,512,128]{2,1,0:T(8,128)(2,1)S(1)} %add_convert_fusion.1._.own_ref), channel_id=1, source_target_pairs={{0,4},{1,5},{2,6},{3,7},{8,12},{9,13},{10,14},{11,15},{16,20},{17,... | collective-permute-start | bytes 1179656 | tf_op jit(solution)/shard_map/ppermute | solution.py:344
  56.4 34.0 %collective-permute-start.19 = (bf16[3,512,128]{2,1,0:T(8,128)(2,1)}, bf16[3,512,128]{2,1,0:T(8,128)(2,1)S(1)}, u32[]{:S(2)}, u32[]{:S(2)}) collective-permute-start(bf16[3,512,128]{2,1,0:T(8,128)(2,1)} %get-tuple-element.41.refs_3_), channel_id=1, source_target_pairs={{4,5},{5,4},{6,7},{7,6},{12,13},{13,12},{14,15},{15,14},{20,21},{2... | collective-permute-start | bytes 1179656 | tf_op jit(solution)/shard_map/ppermute | solution.py:344
  59.8 32.4 %collective-permute-start.20 = (bf16[3,512,128]{2,1,0:T(8,128)(2,1)}, bf16[3,512,128]{2,1,0:T(8,128)(2,1)}, u32[]{:S(2)}, u32[]{:S(2)}) collective-permute-start(bf16[3,512,128]{2,1,0:T(8,128)(2,1)} %get-tuple-element.41.refs_3_), channel_id=1, source_target_pairs={{4,6},{5,7},{6,4},{7,5},{12,14},{13,15},{14,12},{15,13},{20,22},{2... | collective-permute-start | bytes 1179656 | tf_op jit(solution)/shard_map/ppermute | solution.py:344
  77.0 67.8 %collective-permute-start.21 = (bf16[3,512,128]{2,1,0:T(8,128)(2,1)}, bf16[3,512,128]{2,1,0:T(8,128)(2,1)}, u32[]{:S(2)}, u32[]{:S(2)}) collective-permute-start(bf16[3,512,128]{2,1,0:T(8,128)(2,1)} %get-tuple-element.41.refs_3_), channel_id=1, source_target_pairs={{4,7},{5,6},{6,5},{7,4},{12,15},{13,14},{14,13},{15,12},{20,23},{2... | collective-permute-start | bytes 1179656 | tf_op jit(solution)/shard_map/ppermute | solution.py:344
  82.5 142.7 %collective-permute-start.5 = (bf16[2,512,1024]{2,1,0:T(8,128)(2,1)}, bf16[2,512,1024]{2,1,0:T(8,128)(2,1)S(1)}, u32[]{:S(2)}, u32[]{:S(2)}) collective-permute-start(bf16[2,512,1024]{2,1,0:T(8,128)(2,1)} %tail_rows.1), channel_id=1, source_target_pairs={{3,4},{4,5},{5,6},{6,7},{11,12},{12,13},{13,14},{14,15},{19,20},{2... | collective-permute-start | bytes 6291464 | tf_op jit(solution)/shard_map/ppermute | solution.py:344
  85.0 140.6 %collective-permute-start.4 = (bf16[2,512,1024]{2,1,0:T(8,128)(2,1)}, bf16[2,512,1024]{2,1,0:T(8,128)(2,1)}, u32[]{:S(2)}, u32[]{:S(2)}) collective-permute-start(bf16[2,512,1024]{2,1,0:T(8,128)(2,1)} %tail_rows.1), channel_id=1, source_target_pairs={{0,1},{1,2},{2,3},{8,9},{9,10},{10,11},{16,17},{17,18},{18,19},{24... | collective-permute-start | bytes 6291464 | tf_op jit(solution)/shard_map/ppermute | solution.py:344
  90.3 69.2 %collective-permute-start.6 = (bf16[3,512,128]{2,1,0:T(8,128)(2,1)}, bf16[3,512,128]{2,1,0:T(8,128)(2,1)S(1)}, u32[]{:S(2)}, u32[]{:S(2)}) collective-permute-start(bf16[3,512,128]{2,1,0:T(8,128)(2,1)} %get-tuple-element.31.refs_3_), channel_id=1, source_target_pairs={{4,5},{5,4},{6,7},{7,6},{12,13},{13,12},{14,15},{15,14},{20,21},{2... | collective-permute-start | bytes 1179656 | tf_op jit(solution)/shard_map/ppermute | solution.py:344
  92.3 70.5 %collective-permute-start.7 = (bf16[3,512,128]{2,1,0:T(8,128)(2,1)}, bf16[3,512,128]{2,1,0:T(8,128)(2,1)S(1)}, u32[]{:S(2)}, u32[]{:S(2)}) collective-permute-start(bf16[3,512,128]{2,1,0:T(8,128)(2,1)} %get-tuple-element.31.refs_3_), channel_id=1, source_target_pairs={{4,6},{5,7},{6,4},{7,5},{12,14},{13,15},{14,12},{15,13},{20,22},{2... | collective-permute-start | bytes 1179656 | tf_op jit(solution)/shard_map/ppermute | solution.py:344
  144.8 21.4 %collective-permute-start.8 = (bf16[3,512,128]{2,1,0:T(8,128)(2,1)}, bf16[3,512,128]{2,1,0:T(8,128)(2,1)}, u32[]{:S(2)}, u32[]{:S(2)}) collective-permute-start(bf16[3,512,128]{2,1,0:T(8,128)(2,1)} %get-tuple-element.31.refs_3_), channel_id=1, source_target_pairs={{4,7},{5,6},{6,5},{7,4},{12,15},{13,14},{14,13},{15,12},{20,23},{2... | collective-permute-start | bytes 1179656 | tf_op jit(solution)/shard_map/ppermute | solution.py:344
  160.3 20.9 %collective-permute-start.22 = (bf16[3,512,128]{2,1,0:T(8,128)(2,1)}, bf16[3,512,128]{2,1,0:T(8,128)(2,1)S(1)}, u32[]{:S(2)}, u32[]{:S(2)}) collective-permute-start(bf16[3,512,128]{2,1,0:T(8,128)(2,1)} %get-tuple-element.43), channel_id=1, source_target_pairs={{4,5},{5,4},{6,7},{7,6},{12,13},{13,12},{14,15},{15,14},{20,21},{2... | collective-permute-start | bytes 1179656 | tf_op jit(solution)/shard_map/ppermute | solution.py:344
  162.8 22.3 %collective-permute-start.23 = (bf16[3,512,128]{2,1,0:T(8,128)(2,1)}, bf16[3,512,128]{2,1,0:T(8,128)(2,1)S(1)}, u32[]{:S(2)}, u32[]{:S(2)}) collective-permute-start(bf16[3,512,128]{2,1,0:T(8,128)(2,1)} %get-tuple-element.44), channel_id=1, source_target_pairs={{4,6},{5,7},{6,4},{7,5},{12,14},{13,15},{14,12},{15,13},{20,22},{2... | collective-permute-start | bytes 1179656 | tf_op jit(solution)/shard_map/ppermute | solution.py:344
  166.2 20.9 %collective-permute-start.24 = (bf16[3,512,128]{2,1,0:T(8,128)(2,1)}, bf16[3,512,128]{2,1,0:T(8,128)(2,1)S(1)}, u32[]{:S(2)}, u32[]{:S(2)}) collective-permute-start(bf16[3,512,128]{2,1,0:T(8,128)(2,1)} %get-tuple-element.45), channel_id=1, source_target_pairs={{4,7},{5,6},{6,5},{7,4},{12,15},{13,14},{14,13},{15,12},{20,23},{2... | collective-permute-start | bytes 1179656 | tf_op jit(solution)/shard_map/ppermute | solution.py:344
  185.2 18.7 %collective-permute-start.11 = (bf16[3,512,128]{2,1,0:T(8,128)(2,1)}, bf16[3,512,128]{2,1,0:T(8,128)(2,1)}, u32[]{:S(2)}, u32[]{:S(2)}) collective-permute-start(bf16[3,512,128]{2,1,0:T(8,128)(2,1)} %get-tuple-element.35), channel_id=1, source_target_pairs={{4,7},{5,6},{6,5},{7,4},{12,15},{13,14},{14,13},{15,12},{20,23},{2... | collective-permute-start | bytes 1179656 | tf_op jit(solution)/shard_map/ppermute | solution.py:344
  187.1 20.5 %collective-permute-start.9 = (bf16[3,512,128]{2,1,0:T(8,128)(2,1)}, bf16[3,512,128]{2,1,0:T(8,128)(2,1)}, u32[]{:S(2)}, u32[]{:S(2)}) collective-permute-start(bf16[3,512,128]{2,1,0:T(8,128)(2,1)} %get-tuple-element.33), channel_id=1, source_target_pairs={{4,5},{5,4},{6,7},{7,6},{12,13},{13,12},{14,15},{15,14},{20,21},{2... | collective-permute-start | bytes 1179656 | tf_op jit(solution)/shard_map/ppermute | solution.py:344
  194.4 30.6 %collective-permute-start.25 = (bf16[3,512,128]{2,1,0:T(8,128)(2,1)}, bf16[3,512,128]{2,1,0:T(8,128)(2,1)S(1)}, u32[]{:S(2)}, u32[]{:S(2)}) collective-permute-start(bf16[3,512,128]{2,1,0:T(8,128)(2,1)} %renew_second.3.refs_3_), channel_id=1, source_target_pairs={{0,1},{1,0},{2,3},{3,2},{4,5},{5,4},{6,7},{7,6},{8,9},{9,8},{10,11... | collective-permute-start | bytes 1179656 | tf_op jit(solution)/shard_map/ppermute | solution.py:344
  203.9 39.0 %collective-permute-start.26 = (bf16[3,512,128]{2,1,0:T(8,128)(2,1)S(1)}, bf16[3,512,128]{2,1,0:T(8,128)(2,1)S(1)}, u32[]{:S(2)}, u32[]{:S(2)}) collective-permute-start(bf16[3,512,128]{2,1,0:T(8,128)(2,1)S(1)} %copy-done.3), channel_id=1, source_target_pairs={{0,2},{1,3},{2,0},{3,1},{4,6},{5,7},{6,4},{7,5},{8,10},{9,11},{10,... | collective-permute-start | bytes 1179656 | tf_op jit(solution)/shard_map/ppermute | solution.py:344
  207.6 35.2 %collective-permute-start.27 = (bf16[3,512,128]{2,1,0:T(8,128)(2,1)S(1)}, bf16[3,512,128]{2,1,0:T(8,128)(2,1)}, u32[]{:S(2)}, u32[]{:S(2)}) collective-permute-start(bf16[3,512,128]{2,1,0:T(8,128)(2,1)S(1)} %copy-done.3), channel_id=1, source_target_pairs={{0,3},{1,2},{2,1},{3,0},{4,7},{5,6},{6,5},{7,4},{8,11},{9,10},{10,... | collective-permute-start | bytes 1179656 | tf_op jit(solution)/shard_map/ppermute | solution.py:344
  225.0 25.9 %collective-permute-start.12 = (bf16[3,512,128]{2,1,0:T(8,128)(2,1)}, bf16[3,512,128]{2,1,0:T(8,128)(2,1)}, u32[]{:S(2)}, u32[]{:S(2)}) collective-permute-start(bf16[3,512,128]{2,1,0:T(8,128)(2,1)} %renew_second.2.refs_3_), channel_id=1, source_target_pairs={{0,1},{1,0},{2,3},{3,2},{4,5},{5,4},{6,7},{7,6},{8,9},{9,8},{10,11... | collective-permute-start | bytes 1179656 | tf_op jit(solution)/shard_map/ppermute | solution.py:344
  225.2 25.7 %collective-permute-start.13 = (bf16[3,512,128]{2,1,0:T(8,128)(2,1)}, bf16[3,512,128]{2,1,0:T(8,128)(2,1)}, u32[]{:S(2)}, u32[]{:S(2)}) collective-permute-start(bf16[3,512,128]{2,1,0:T(8,128)(2,1)} %renew_second.2.refs_3_), channel_id=1, source_target_pairs={{0,2},{1,3},{2,0},{3,1},{4,6},{5,7},{6,4},{7,5},{8,10},{9,11},{10,... | collective-permute-start | bytes 1179656 | tf_op jit(solution)/shard_map/ppermute | solution.py:344
  225.6 25.3 %collective-permute-start.14 = (bf16[3,512,128]{2,1,0:T(8,128)(2,1)}, bf16[3,512,128]{2,1,0:T(8,128)(2,1)}, u32[]{:S(2)}, u32[]{:S(2)}) collective-permute-start(bf16[3,512,128]{2,1,0:T(8,128)(2,1)} %renew_second.2.refs_3_), channel_id=1, source_target_pairs={{0,3},{1,2},{2,1},{3,0},{4,7},{5,6},{6,5},{7,4},{8,11},{9,10},{10,... | collective-permute-start | bytes 1179656 | tf_op jit(solution)/shard_map/ppermute | solution.py:344
  (20 other events, 201.4 us)
where the time goes:
time: 259 us; the launch traced here: 258 us
  starting transfers between devices  121 us (47%)
  Pallas kernels  110 us (42%)
  waiting for transfers between devices  23.4 us (9%)
    ppermute x28, starting transfers between devices, hop(): return lax.ppermute(x, 'seq', route)  121 us
    pallas_call x4, Pallas kernels, grads(): pl.pallas_call(functools.partial(grads_kernel, parts, whole, head), out_s...  46.4 us
    ppermute x28, waiting for transfers between devices, hop(): return lax.ppermute(x, 'seq', route)  23.4 us
    pallas_call x2, Pallas kernels, inner_attention(): pl.pallas_call(inner_kernel, out_shape=jax.ShapeDtypeStruct((rows - WINDO...  17.9 us
    pallas_call x2, Pallas kernels, apply_fast(): pl.pallas_call(functools.partial(apply_kernel, parts), out_shape=jax.Shap...  14.7 us
    pallas_call x2, Pallas kernels, edge_attention(): pl.pallas_call(functools.partial(edge_kernel, side), out_shape=jax.ShapeD...  14.3 us
    pallas_call x2, Pallas kernels, renew_second(): pl.pallas_call(renew_second_kernel, out_shape=jax.ShapeDtypeStruct(weight...  7.04 us
    pallas_call x2, Pallas kernels, renew_first(): pl.pallas_call(renew_first_kernel, out_shape=[jax.ShapeDtypeStruct(own.sh...  6.74 us
  transfers between devices with their start and end apart: 28, of which 3 were waited for; matrix products, arithmetic and copies ran while one was open for 0% of the time, Pallas kernels for 35%

commit v1 on v0

--- a/solution.py
+++ b/solution.py
@@ -12,6 +12,7 @@
 AH = 128
 WINDOW = 512
 EPSILON = 1e-06
+GRANT = 28 * 2**20
 F32 = jnp.float32
 BF16 = jnp.bfloat16
 
@@ -106,28 +107,28 @@
             bytes_accessed=4 * rows * hw + 12 * hw * hw,
             transcendentals=rows * hw,
         ),
-        name="grads",
     )(pos, keys, values, rates, *weights)
 
 
-def tail_kernel(k_ref, v_ref, o_ref):
-    o_ref[0] = k_ref[...]
-    o_ref[1] = v_ref[...]
-
-
-def tail_rows(keys, values, step=256):
+def tail_kernel(k_ref, v_ref, main_ref, rest_ref):
+    cut = main_ref.shape[-1]
+    for m, ref in enumerate((k_ref, v_ref)):
+        main_ref[m] = ref[:, :cut]
+        rest_ref[m] = ref[:, cut:]
+
+
+def tail_rows(keys, values, kept, step=256):
     rows, cols = keys.shape
     first = (rows - WINDOW) // step
     spec = pl.BlockSpec((step, cols), lambda i: (first + i, 0))
     return pl.pallas_call(
         tail_kernel,
-        out_shape=jax.ShapeDtypeStruct((2, WINDOW, cols), BF16),
+        out_shape=[jax.ShapeDtypeStruct((2, WINDOW, w), BF16) for w in (kept, cols - kept)],
         grid=(WINDOW // step,),
         in_specs=[spec, spec],
-        out_specs=pl.BlockSpec((2, step, cols), lambda i: (0, i, 0)),
+        out_specs=[pl.BlockSpec((2, step, w), lambda i: (0, i, 0)) for w in (kept, cols - kept)],
         compiler_params=pltpu.CompilerParams(dimension_semantics=("arbitrary",)),
         cost_estimate=pl.CostEstimate(flops=0, bytes_accessed=8 * WINDOW * cols, transcendentals=0),
-        name="tail_rows",
     )(keys, values)
 
 
@@ -160,7 +161,6 @@
             out_specs=[whole, whole],
         ),
         cost_estimate=pl.CostEstimate(flops=18 * hw * width, bytes_accessed=40 * hw * width, transcendentals=0),
-        name="renew_first",
     )(pos, own, far, gate, up, down)
 
 
@@ -185,7 +185,6 @@
             num_scalar_prefetch=1, grid=(1,), in_specs=[whole] * (len(terms) + 1), out_specs=whole
         ),
         cost_estimate=pl.CostEstimate(flops=24 * hw * width, bytes_accessed=40 * hw * width, transcendentals=0),
-        name="renew_second",
     )(pos, *terms, weight)
 
 
@@ -231,11 +230,10 @@
             bytes_accessed=count * rows * AH * 10,
             transcendentals=count * rows * WINDOW,
         ),
-        name="inner_attention",
     )(queries, keys, values, after)
 
 
-def edge_kernel(side, pos_ref, q_ref, k_ref, v_ref, h_ref, *refs):
+def edge_kernel(side, kept, pos_ref, q_ref, k_ref, v_ref, main_ref, rest_ref, relay_ref, *refs):
     o_ref = refs[-1]
     half = WINDOW // 2
     active = pos_ref[1] == side
@@ -243,8 +241,10 @@
     @pl.when(active)
     def _():
         first = pos_ref[2] == 0
-        keys = [h_ref[0, :half], h_ref[0, half:], k_ref[:half, :], k_ref[half:, :]]
-        values = [h_ref[1, :half], h_ref[1, half:], v_ref[:half, :], v_ref[half:, :]]
+        rest = jnp.where(pos_ref[0] == 0, relay_ref[...], rest_ref[...])
+        halo = jnp.where(pl.program_id(0) < kept, main_ref[...], rest)
+        keys = [halo[0, :half], halo[0, half:], k_ref[:half, :], k_ref[half:, :]]
+        values = [halo[1, :half], halo[1, half:], v_ref[:half, :], v_ref[half:, :]]
         for t in range(2):
             outside = [first if j + t < 2 else None for j in range(3)]
             o_ref[t * half : (t + 1) * half, :] = attend_tile(
@@ -256,29 +256,34 @@
         o_ref[...] = refs[0][...] if len(refs) > 1 else jnp.zeros_like(o_ref)
 
 
-def edge_attention(pos, queries, keys, values, halo, before, side):
+def edge_attention(pos, queries, keys, values, main, rest, relay, before, side):
     count = queries.shape[1] // AH
+    kept = main.shape[-1] // AH
     strip = pl.BlockSpec((WINDOW, AH), lambda a, p: (0, jnp.where(p[1] == side, a, 0)))
-    return pl.pallas_call(
-        functools.partial(edge_kernel, side),
+    main_spec = pl.BlockSpec(
+        (2, WINDOW, AH), lambda a, p: (0, 0, jnp.where(p[1] == side, jnp.minimum(a, kept - 1), 0))
+    )
+    rest_spec = pl.BlockSpec(
+        (2, WINDOW, AH), lambda a, p: (0, 0, jnp.where(p[1] == side, jnp.maximum(a - kept, 0), 0))
+    )
+    return pl.pallas_call(
+        functools.partial(edge_kernel, side, kept),
         out_shape=jax.ShapeDtypeStruct((WINDOW, count * AH), BF16),
         grid_spec=pltpu.PrefetchScalarGridSpec(
             num_scalar_prefetch=1,
             grid=(count,),
-            in_specs=[strip, strip, strip]
-            + [pl.BlockSpec((2, WINDOW, AH), lambda a, p: (0, 0, jnp.where(p[1] == side, a, 0)))]
+            in_specs=[strip, strip, strip, main_spec, rest_spec, rest_spec]
             + [pl.BlockSpec((WINDOW, AH), lambda a, p: (0, 0))] * len(before),
             out_specs=strip,
         ),
-        input_output_aliases={5: 0} if before else {},
+        input_output_aliases={7: 0} if before else {},
         compiler_params=pltpu.CompilerParams(dimension_semantics=("arbitrary",)),
         cost_estimate=pl.CostEstimate(
             flops=count * WINDOW * WINDOW * AH * 6,
             bytes_accessed=count * WINDOW * AH * 18,
             transcendentals=count * WINDOW * WINDOW,
         ),
-        name="edge_attention",
-    )(pos, queries, keys, values, halo, *before)
+    )(pos, queries, keys, values, main, rest, relay, *before)
 
 
 def apply_kernel(parts, pos_ref, *refs):
@@ -332,20 +337,32 @@
             scratch_shapes=[pltpu.VMEM((3, hw, hw), BF16)],
         ),
         input_output_aliases=aliases,
-        compiler_params=pltpu.CompilerParams(dimension_semantics=("arbitrary",)),
+        compiler_params=pltpu.CompilerParams(dimension_semantics=("arbitrary",), vmem_limit_bytes=GRANT),
         cost_estimate=pl.CostEstimate(
             flops=6 * rows * hw * hw, bytes_accessed=8 * rows * hw + 6 * hw * hw, transcendentals=rows * hw
         ),
-        name="apply_fast",
     )(*operands)
 
 
-def hop(x, route):
-    return lax.ppermute(x, "seq", route)
+def hop(x, route, axes="seq"):
+    return lax.ppermute(x, axes, route)
 
 
 def spread(xs, low, high):
-    return [hop(x, [(i, i ^ d) for i in range(low, high)]) for d, x in enumerate(xs) if d]
+    rows, cols = lax.axis_size("head"), lax.axis_size("seq")
+    got = []
+    for d, x in enumerate(xs):
+        if d == 0:
+            continue
+        route = []
+        for h in range(rows):
+            for i in range(cols):
+                if low <= i < high:
+                    route.append((h * cols + i, h * cols + (i ^ d)))
+                elif rows % 2 == 0:
+                    route.append((h * cols + i, (h ^ 1) * cols + i))
+        got.append(hop(x, route, ("head", "seq")))
+    return got
 
 
 def fast_device(queries, key_rows, value_rows, learn_rates, gate_fast, down_fast, up_fast):
@@ -362,9 +379,17 @@
     first_w = (gate_fast, up_fast, down_fast)
     span = range(heads)
 
-    tail = tail_rows(key_rows, value_rows)
-    halo_a = hop(tail, early)
+    count = queries.shape[1] // AH
+    main, rest = tail_rows(key_rows, value_rows, (count - count // 4) * AH)
+    side_a = hop(rest, [(parts - 1, parts - 2)])
+    main_a = hop(main, early)
+    rest_a = hop(rest, early[1:])
+    relay_a = hop(side_a, [(parts - 2, parts)])
     terms = [grads(pos, h, parts, key_rows, value_rows, rates, first_w, True) for h in span]
+
+    def attend_inner(h, after):
+        inner.append(inner_attention(queries, key_rows, value_rows, h * per_head, per_head, after))
+
     shards, w1, far, inner = [], [], [], []
     for h in span:
         got = spread(terms[h], 0, parts)
@@ -373,20 +398,24 @@
             own = own + g.astype(F32)
         own = own.astype(BF16)
         far.append(hop(own, across))
-        inner.append(inner_attention(queries, key_rows, value_rows, h * per_head, per_head, own))
+        if h == 0:
+            attend_inner(h, own)
         shard, shard_bf = renew_first(pos, h, own, far[h], *first_w)
         shards.append(shard)
         w1.append([shard_bf] + spread([shard_bf] * parts, parts, seq_count))
-    edge = edge_attention(pos, queries, key_rows, value_rows, halo_a, (), 1)
-    tail, _ = lax.optimization_barrier((tail, far[-1]))
-    halo_b = hop(tail, late)
+    edge = edge_attention(pos, queries, key_rows, value_rows, main_a, rest_a, relay_a, (), 1)
+    (main, rest), _ = lax.optimization_barrier(((main, rest), own))
+    main_b = hop(main, late)
+    rest_b = hop(rest, late)
     w2 = []
     for h in span:
         term = grads(pos, h, parts, key_rows, value_rows, rates, w1[h], False)
         got = [term[0]] + spread(term, parts, seq_count)
         shard_bf = renew_second(pos, got, shards[h])
+        if h:
+            attend_inner(h, w2[h - 1][0])
         w2.append([shard_bf] + spread([shard_bf] * parts, 0, seq_count))
-    edge = edge_attention(pos, queries, key_rows, value_rows, halo_b, (edge,), 0)
+    edge = edge_attention(pos, queries, key_rows, value_rows, main_b, rest_b, rest_b, (edge,), 0)
     out = None
     for h in span:
         out = apply_fast(pos, h, queries, edge, inner[h], w2[h], out)
@@ -518,7 +547,13 @@
 
     def fits(args):
         width = args[4].shape[1] // parts
-        return parts & (parts - 1) == 0 and width % AH == 0 and args[0].shape[0] >= 2 * WINDOW
+        return (
+            parts & (parts - 1) == 0
+            and parts > 1
+            and width % AH == 0
+            and args[0].shape[0] >= 2 * WINDOW
+            and args[0].shape[1] >= 4 * AH
+        )
 
     def on_device(*args):
         if fits(args):

time: 259 us -> 243 us (0.938)
  starting transfers between devices: 121 us -> 33.5 us
  waiting for transfers between devices: 23.4 us -> 89.9 us
  local copies, waits for them, and re-layouts: 2.28 us -> 6.56 us
    ppermute x28 -> x32, starting transfers between devices: 121 us -> 33.5 us  [hop(): return lax.ppermute(x, axes, route)]
    ppermute x28 -> x32, waiting for transfers between devices: 23.4 us -> 89.9 us  [hop(): return lax.ppermute(x, axes, route)]
    unnamed x32 -> x52, local copies, waits for them, and re-layouts: 2.28 us -> 6.56 us
  transfers between devices with their start and end apart: 28 -> 32, of which waited for: 3 -> 7; matrix products, arithmetic and copies ran while one was open for 0% -> 1% of each run, Pallas kernels for 35% -> 38%
where the time goes in v1:
time: 243 us; the launch traced here: 242 us
  Pallas kernels  109 us (45%)
  waiting for transfers between devices  89.9 us (37%)
  starting transfers between devices  33.5 us (14%)
  local copies, waits for them, and re-layouts  6.56 us (3%)
    ppermute x32, waiting for transfers between devices, hop(): return lax.ppermute(x, axes, route)  89.9 us
    pallas_call x4, Pallas kernels, grads(): pl.pallas_call(functools.partial(grads_kernel, parts, whole, head), out_s...  46.6 us
    ppermute x32, starting transfers between devices, hop(): return lax.ppermute(x, axes, route)  33.5 us
    pallas_call x2, Pallas kernels, inner_attention(): pl.pallas_call(inner_kernel, out_shape=jax.ShapeDtypeStruct((rows - WINDO...  18 us
    pallas_call x2, Pallas kernels, edge_attention(): pl.pallas_call(functools.partial(edge_kernel, side, kept), out_shape=jax....  15.3 us
    pallas_call x2, Pallas kernels, apply_fast(): pl.pallas_call(functools.partial(apply_kernel, parts), out_shape=jax.Shap...  13.2 us
    pallas_call x2, Pallas kernels, renew_second(): pl.pallas_call(renew_second_kernel, out_shape=jax.ShapeDtypeStruct(weight...  6.96 us
    pallas_call x2, Pallas kernels, renew_first(): pl.pallas_call(renew_first_kernel, out_shape=[jax.ShapeDtypeStruct(own.sh...  6.73 us
  transfers between devices with their start and end apart: 32, of which 7 were waited for; matrix products, arithmetic and copies ran while one was open for 1% of the time, Pallas kernels for 38%

profile of v1, /device:TPU:26, one launch (start us, length us, event | category | flops | bytes accessed | tf_op | source)
XLA Modules:
  0.0 241.6 jit_solution(6842685070807024643)
XLA Ops:
  0.6 11.8 %shard_map.77 = (bf16[3,512,128]{2,1,0:T(8,128)(2,1)}, bf16[3,512,128]{2,1,0:T(8,128)(2,1)}, bf16[3,512,128]{2,1,0:T(8,128)(2,1)}, bf16[3,512,128]{2,1,0:T(8,128)(2,1)}) custom-call(s32[3]{0:T(128)} %pad_add_fusion.pos_ref, bf16[1536,1024]{1,0:T(8,128)(2,1)} %k_ref.9, bf16[1536,1024]{1,0:T(8,128)(2,1)} %v_ref.9, bf16[2,1536]{1,0:T(2,128)(2,1)} %bitcast.4, ...), custom_call_target="tpu_custom_call" | custom-call | flops 4831838208 | bytes 6291456 | tf_op jit(solution)/shard_map/pallas_call | solution.py:93
  12.9 11.7 %shard_map.74 = (bf16[3,512,128]{2,1,0:T(8,128)(2,1)}, bf16[3,512,128]{2,1,0:T(8,128)(2,1)}, bf16[3,512,128]{2,1,0:T(8,128)(2,1)}, bf16[3,512,128]{2,1,0:T(8,128)(2,1)}) custom-call(s32[3]{0:T(128)} %pad_add_fusion.pos_ref, bf16[1536,1024]{1,0:T(8,128)(2,1)} %k_ref.9, bf16[1536,1024]{1,0:T(8,128)(2,1)} %v_ref.9, bf16[2,1536]{1,0:T(2,128)(2,1)} %bitcast.5, ...), custom_call_target="tpu_custom_call" | custom-call | flops 4831838208 | bytes 6291456 | tf_op jit(solution)/shard_map/pallas_call | solution.py:93
  25.7 2.6 %shard_map.73 = (bf16[2,512,768]{2,1,0:T(8,128)(2,1)}, bf16[2,512,256]{2,1,0:T(8,128)(2,1)}) custom-call(bf16[1536,1024]{1,0:T(8,128)(2,1)} %k_ref.9, bf16[1536,1024]{1,0:T(8,128)(2,1)} %v_ref.9), custom_call_target="tpu_custom_call" | custom-call | bytes 4194304 | tf_op jit(solution)/shard_map/pallas_call | solution.py:124
  29.9 3.4 %collective-permute-start.6 = (bf16[2,512,256]{2,1,0:T(8,128)(2,1)}, bf16[2,512,256]{2,1,0:T(8,128)(2,1)S(1)}, u32[]{:S(2)}, u32[]{:S(2)}) collective-permute-start(bf16[2,512,256]{2,1,0:T(8,128)(2,1)} %get-tuple-element.36), channel_id=1, source_target_pairs={{4,5},{5,6},{6,7},{12,13},{13,14},{14,15},{20,21},{21,22},{22,23},... | collective-permute-start | bytes 1572872 | tf_op jit(solution)/shard_map/ppermute | solution.py:348
  39.6 34.3 %collective-permute-done.12.far_ref = bf16[3,512,128]{2,1,0:T(8,128)(2,1)S(1)} collective-permute-done((bf16[3,512,128]{2,1,0:T(8,128)(2,1)S(1)}, bf16[3,512,128]{2,1,0:T(8,128)(2,1)S(1)}, u32[]{:S(2)}, u32[]{:S(2)}) %collective-permute-start.12) | collective-permute-done | bytes 393248 | tf_op jit(solution)/shard_map/ppermute | solution.py:348
  74.7 3.4 %shard_map.78 = (f32[3,512,128]{2,1,0:T(8,128)}, bf16[3,512,128]{2,1,0:T(8,128)(2,1)}) custom-call(s32[3]{0:T(128)} %pad_add_fusion.pos_ref, bf16[3,512,128]{2,1,0:T(8,128)(2,1)} %copy-done.8, bf16[3,512,128]{2,1,0:T(8,128)(2,1)} %copy-done.14, f32[2,512,512]{2,1,0:T(8,128)} %g_ref.3, f32[2,512,512]{2,1,0:T(8,128)} %u_ref.3, f32[2,512,512]{2,1,0:T(8,128)} %d_ref.3), custom_call_target="tpu_custom_call" | custom-call | flops 1179648 | bytes 2621440 | tf_op jit(solution)/shard_map/pallas_call | solution.py:154
  79.5 2.9 %collective-permute-done.19.far_ref = bf16[3,512,128]{2,1,0:T(8,128)(2,1)S(1)} collective-permute-done((bf16[3,512,128]{2,1,0:T(8,128)(2,1)S(1)}, bf16[3,512,128]{2,1,0:T(8,128)(2,1)S(1)}, u32[]{:S(2)}, u32[]{:S(2)}) %collective-permute-start.19) | collective-permute-done | bytes 393248 | tf_op jit(solution)/shard_map/ppermute | solution.py:348
  83.1 3.4 %shard_map.82 = (f32[3,512,128]{2,1,0:T(8,128)}, bf16[3,512,128]{2,1,0:T(8,128)(2,1)}) custom-call(s32[3]{0:T(128)} %pad_add_fusion.pos_ref, bf16[3,512,128]{2,1,0:T(8,128)(2,1)} %copy-done.10, bf16[3,512,128]{2,1,0:T(8,128)(2,1)} %copy-done.13, f32[2,512,512]{2,1,0:T(8,128)} %g_ref.3, f32[2,512,512]{2,1,0:T(8,128)} %u_ref.3, f32[2,512,512]{2,1,0:T(8,128)} %d_ref.3), custom_call_target="tpu_custom_call" | custom-call | flops 1179648 | bytes 2621440 | tf_op jit(solution)/shard_map/pallas_call | solution.py:154
  90.2 35.3 %collective-permute-done.13.refs_4_ = bf16[3,512,128]{2,1,0:T(8,128)(2,1)S(1)} collective-permute-done((bf16[3,512,128]{2,1,0:T(8,128)(2,1)}, bf16[3,512,128]{2,1,0:T(8,128)(2,1)S(1)}, u32[]{:S(2)}, u32[]{:S(2)}) %collective-permute-start.13) | collective-permute-done | bytes 393248 | tf_op jit(solution)/shard_map/ppermute | solution.py:348
  125.6 3.4 %collective-permute-start.22 = (bf16[3,512,128]{2,1,0:T(8,128)(2,1)}, bf16[3,512,128]{2,1,0:T(8,128)(2,1)}, u32[]{:S(2)}, u32[]{:S(2)}) collective-permute-start(bf16[3,512,128]{2,1,0:T(8,128)(2,1)} %get-tuple-element.47.refs_3_), channel_id=1, source_target_pairs={{0,8},{1,9},{2,10},{3,11},{4,7},{5,6},{6,5},{7,4},{8,0},{9,1},{10,... | collective-permute-start | bytes 1179656 | tf_op jit(solution)/shard_map/ppermute | solution.py:348
  129.0 11.6 %shard_map.79 = (bf16[3,512,128]{2,1,0:T(8,128)(2,1)}, bf16[3,512,128]{2,1,0:T(8,128)(2,1)}, bf16[3,512,128]{2,1,0:T(8,128)(2,1)}, bf16[3,512,128]{2,1,0:T(8,128)(2,1)}) custom-call(s32[3]{0:T(128)} %pad_add_fusion.pos_ref, bf16[1536,1024]{1,0:T(8,128)(2,1)} %k_ref.9, bf16[1536,1024]{1,0:T(8,128)(2,1)} %v_ref.9, bf16[2,1536]{1,0:T(2,128)(2,1)} %bitcast.6, ...), custom_call_target="tpu_custom_call" | custom-call | flops 4831838208 | bytes 6291456 | tf_op jit(solution)/shard_map/pallas_call | solution.py:93
  140.6 3.5 %collective-permute-done.20.refs_4_ = bf16[3,512,128]{2,1,0:T(8,128)(2,1)} collective-permute-done((bf16[3,512,128]{2,1,0:T(8,128)(2,1)}, bf16[3,512,128]{2,1,0:T(8,128)(2,1)}, u32[]{:S(2)}, u32[]{:S(2)}) %collective-permute-start.20) | collective-permute-done | bytes 393248 | tf_op jit(solution)/shard_map/ppermute | solution.py:348
  144.1 2.5 %collective-permute-start.16 = (bf16[3,512,128]{2,1,0:T(8,128)(2,1)}, bf16[3,512,128]{2,1,0:T(8,128)(2,1)S(1)}, u32[]{:S(2)}, u32[]{:S(2)}) collective-permute-start(bf16[3,512,128]{2,1,0:T(8,128)(2,1)} %get-tuple-element.43), channel_id=1, source_target_pairs={{0,8},{1,9},{2,10},{3,11},{4,5},{5,4},{6,7},{7,6},{8,0},{9,1},{10,... | collective-permute-start | bytes 1179656 | tf_op jit(solution)/shard_map/ppermute | solution.py:348
  148.1 11.5 %shard_map.83 = (bf16[3,512,128]{2,1,0:T(8,128)(2,1)}, bf16[3,512,128]{2,1,0:T(8,128)(2,1)}, bf16[3,512,128]{2,1,0:T(8,128)(2,1)}, bf16[3,512,128]{2,1,0:T(8,128)(2,1)}) custom-call(s32[3]{0:T(128)} %pad_add_fusion.pos_ref, bf16[1536,1024]{1,0:T(8,128)(2,1)} %k_ref.9, bf16[1536,1024]{1,0:T(8,128)(2,1)} %v_ref.9, bf16[2,1536]{1,0:T(2,128)(2,1)} %bitcast.7, ...), custom_call_target="tpu_custom_call" | custom-call | flops 4831838208 | bytes 6291456 | tf_op jit(solution)/shard_map/pallas_call | solution.py:93
  162.1 4.2 %collective-permute-done.18.refs_3_ = bf16[3,512,128]{2,1,0:T(8,128)(2,1)S(1)} collective-permute-done((bf16[3,512,128]{2,1,0:T(8,128)(2,1)}, bf16[3,512,128]{2,1,0:T(8,128)(2,1)S(1)}, u32[]{:S(2)}, u32[]{:S(2)}) %collective-permute-start.18) | collective-permute-done | bytes 393248 | tf_op jit(solution)/shard_map/ppermute | solution.py:348
  167.6 3.5 %shard_map.80._.refs_3_ = bf16[3,512,128]{2,1,0:T(8,128)(2,1)} custom-call(s32[3]{0:T(128)} %pad_add_fusion.pos_ref, bf16[3,512,128]{2,1,0:T(8,128)(2,1)} %get-tuple-element.42.refs_0_, bf16[3,512,128]{2,1,0:T(8,128)(2,1)} %copy-done.18, bf16[3,512,128]{2,1,0:T(8,128)(2,1)} %copy-done.20, bf16[3,512,128]{2,1,0:T(8,128)(2,1)} %copy-done.22, ...), custom_call_target="tpu_custom_call" | custom-call | flops 1572864 | bytes 2621440 | tf_op jit(solution)/shard_map/pallas_call | solution.py:181
  171.1 9.2 %collective-permute-done.23.refs_1_ = bf16[3,512,128]{2,1,0:T(8,128)(2,1)S(1)} collective-permute-done((bf16[3,512,128]{2,1,0:T(8,128)(2,1)}, bf16[3,512,128]{2,1,0:T(8,128)(2,1)S(1)}, u32[]{:S(2)}, u32[]{:S(2)}) %collective-permute-start.23) | collective-permute-done | bytes 393248 | tf_op jit(solution)/shard_map/ppermute | solution.py:348
  181.7 9.0 %shard_map.85.refs_2_ = bf16[1024,512]{1,0:T(8,128)(2,1)} custom-call(bf16[1536,1024]{1,0:T(8,128)(2,1)} %refs_0_.11, bf16[1536,1024]{1,0:T(8,128)(2,1)} %k_ref.9, bf16[1536,1024]{1,0:T(8,128)(2,1)} %v_ref.9, bf16[3,512,128]{2,1,0:T(8,128)(2,1)} %copy-done.8), custom_call_target="tpu_custom_call" | custom-call | flops 2415919104 | bytes 7864320 | tf_op jit(solution)/shard_map/pallas_call | solution.py:221
  192.8 9.0 %shard_map.81.refs_2_ = bf16[1024,512]{1,0:T(8,128)(2,1)} custom-call(bf16[1536,1024]{1,0:T(8,128)(2,1)} %refs_0_.11, bf16[1536,1024]{1,0:T(8,128)(2,1)} %k_ref.9, bf16[1536,1024]{1,0:T(8,128)(2,1)} %v_ref.9, bf16[3,512,128]{2,1,0:T(8,128)(2,1)} %shard_map.80._.refs_3_), custom_call_target="tpu_custom_call" | custom-call | flops 2415919104 | bytes 7864320 | tf_op jit(solution)/shard_map/pallas_call | solution.py:221
  201.9 3.5 %shard_map.84.refs_3_ = bf16[3,512,128]{2,1,0:T(8,128)(2,1)} custom-call(s32[3]{0:T(128)} %pad_add_fusion.pos_ref, bf16[3,512,128]{2,1,0:T(8,128)(2,1)} %get-tuple-element.48.refs_0_, bf16[3,512,128]{2,1,0:T(8,128)(2,1)} %copy-done.16, bf16[3,512,128]{2,1,0:T(8,128)(2,1)} %copy-done.19, bf16[3,512,128]{2,1,0:T(8,128)(2,1)} %copy-done.21, ...), custom_call_target="tpu_custom_call" | custom-call | flops 1572864 | bytes 2621440 | tf_op jit(solution)/shard_map/pallas_call | solution.py:181
  209.6 11.4 %shard_map.75.refs_0_ = bf16[512,1024]{1,0:T(8,128)(2,1)} custom-call(s32[3]{0:T(128)} %pad_add_fusion.pos_ref, bf16[1536,1024]{1,0:T(8,128)(2,1)} %refs_0_.11, bf16[1536,1024]{1,0:T(8,128)(2,1)} %k_ref.9, bf16[1536,1024]{1,0:T(8,128)(2,1)} %v_ref.9, bf16[2,512,768]{2,1,0:T(8,128)(2,1)} %copy-done.11, bf16[2,512,256]{2,1,0:T(8,128)(2,1)} %copy-done.12, ...), custom_call_target="tpu_custom_call" | custom-call | flops 1610612736 | bytes 9437184 | tf_op jit(solution)/shard_map/pallas_call | solution.py:269
  221.0 3.9 %shard_map.76.refs_1_ = bf16[512,1024]{1,0:T(8,128)(2,1)} custom-call(s32[3]{0:T(128)} %pad_add_fusion.pos_ref, bf16[1536,1024]{1,0:T(8,128)(2,1)} %refs_0_.11, bf16[1536,1024]{1,0:T(8,128)(2,1)} %k_ref.9, bf16[1536,1024]{1,0:T(8,128)(2,1)} %v_ref.9, bf16[2,512,768]{2,1,0:T(8,128)(2,1)} %collective-permute-done.3.main_ref, ...), custom_call_target="tpu_custom_call", output_to_operand_aliasing={{}: (7, {})} | custom-call | flops 1610612736 | bytes 9437184 | tf_op jit(solution)/shard_map/pallas_call | solution.py:269
  228.4 6.6 %shard_map.86.refs_7_ = bf16[1536,1024]{1,0:T(8,128)(2,1)} custom-call(s32[3]{0:T(128)S(1)} %copy-done.7, bf16[1536,1024]{1,0:T(8,128)(2,1)S(1)} %copy-done, bf16[512,1024]{1,0:T(8,128)(2,1)S(1)} %copy-done.1, bf16[1024,512]{1,0:T(8,128)(2,1)S(1)} %copy-done.2, bf16[3,512,128]{2,1,0:T(8,128)(2,1)} %shard_map.80._.refs_3_, ...), custom_call_target="tpu_custom_call" | custom-call | flops 2415919104 | bytes 7864320 | tf_op jit(solution)/shard_map/pallas_call | solution.py:329
  235.0 6.6 %shard_map.87 = bf16[1536,1024]{1,0:T(8,128)(2,1)} custom-call(s32[3]{0:T(128)S(1)} %copy-done.7, bf16[1536,1024]{1,0:T(8,128)(2,1)S(1)} %copy-done, bf16[512,1024]{1,0:T(8,128)(2,1)S(1)} %copy-done.1, bf16[1024,512]{1,0:T(8,128)(2,1)S(1)} %copy-done.3, bf16[3,512,128]{2,1,0:T(8,128)(2,1)S(1)} %copy-done.4, ...), custom_call_target="tpu_custom_call", output_to_operand_aliasing={{}: (8, {})} | custom-call | flops 2415919104 | bytes 7864320 | tf_op jit(solution)/shard_map/pallas_call | solution.py:329
  (110 shorter events, 33.3 us)
Async XLA Ops:
  12.9 17.0 %collective-permute-start.9 = (bf16[3,512,128]{2,1,0:T(8,128)(2,1)}, bf16[3,512,128]{2,1,0:T(8,128)(2,1)S(1)}, u32[]{:S(2)}, u32[]{:S(2)}) collective-permute-start(bf16[3,512,128]{2,1,0:T(8,128)(2,1)} %get-tuple-element.38), channel_id=1, source_target_pairs={{0,1},{1,0},{2,3},{3,2},{4,12},{5,13},{6,14},{7,15},{8,9},{9,8},{1... | collective-permute-start | bytes 1179656 | tf_op jit(solution)/shard_map/ppermute | solution.py:348
  29.9 49.6 %collective-permute-start.6 = (bf16[2,512,256]{2,1,0:T(8,128)(2,1)}, bf16[2,512,256]{2,1,0:T(8,128)(2,1)S(1)}, u32[]{:S(2)}, u32[]{:S(2)}) collective-permute-start(bf16[2,512,256]{2,1,0:T(8,128)(2,1)} %get-tuple-element.36), channel_id=1, source_target_pairs={{4,5},{5,6},{6,7},{12,13},{13,14},{14,15},{20,21},{21,22},{22,23},... | collective-permute-start | bytes 1572872 | tf_op jit(solution)/shard_map/ppermute | solution.py:348
  33.6 40.4 %collective-permute-start.12 = (bf16[3,512,128]{2,1,0:T(8,128)(2,1)S(1)}, bf16[3,512,128]{2,1,0:T(8,128)(2,1)S(1)}, u32[]{:S(2)}, u32[]{:S(2)}) collective-permute-start(bf16[3,512,128]{2,1,0:T(8,128)(2,1)S(1)} %add_convert_fusion.own_ref._), channel_id=1, source_target_pairs={{0,4},{1,5},{2,6},{3,7},{8,12},{9,13},{10,14},{11,15},{16,20},{17,... | collective-permute-start | bytes 1179656 | tf_op jit(solution)/shard_map/ppermute | solution.py:348
  36.1 46.2 %collective-permute-start.19 = (bf16[3,512,128]{2,1,0:T(8,128)(2,1)S(1)}, bf16[3,512,128]{2,1,0:T(8,128)(2,1)S(1)}, u32[]{:S(2)}, u32[]{:S(2)}) collective-permute-start(bf16[3,512,128]{2,1,0:T(8,128)(2,1)S(1)} %add_convert_fusion.1.own_ref), channel_id=1, source_target_pairs={{0,4},{1,5},{2,6},{3,7},{8,12},{9,13},{10,14},{11,15},{16,20},{17,... | collective-permute-start | bytes 1179656 | tf_op jit(solution)/shard_map/ppermute | solution.py:348
  37.4 49.0 %collective-permute-start.4 = (bf16[2,512,256]{2,1,0:T(8,128)(2,1)}, bf16[2,512,256]{2,1,0:T(8,128)(2,1)S(1)}, u32[]{:S(2)}, u32[]{:S(2)}) collective-permute-start(bf16[2,512,256]{2,1,0:T(8,128)(2,1)} %get-tuple-element.36), channel_id=1, source_target_pairs={{0,1},{1,2},{2,3},{8,9},{9,10},{10,11},{16,17},{17,18},{18,19},{24... | collective-permute-start | bytes 1572872 | tf_op jit(solution)/shard_map/ppermute | solution.py:348
  38.1 50.3 %collective-permute-start.8 = (bf16[2,512,256]{2,1,0:T(8,128)(2,1)}, bf16[2,512,256]{2,1,0:T(8,128)(2,1)}, u32[]{:S(2)}, u32[]{:S(2)}) collective-permute-start(bf16[2,512,256]{2,1,0:T(8,128)(2,1)} %collective-permute-done.7), channel_id=1, source_target_pairs={{2,4},{10,12},{18,20},{26,28}} | collective-permute-start | bytes 1572872 | tf_op jit(solution)/shard_map/ppermute | solution.py:348
  78.1 47.4 %collective-permute-start.13 = (bf16[3,512,128]{2,1,0:T(8,128)(2,1)}, bf16[3,512,128]{2,1,0:T(8,128)(2,1)S(1)}, u32[]{:S(2)}, u32[]{:S(2)}) collective-permute-start(bf16[3,512,128]{2,1,0:T(8,128)(2,1)} %get-tuple-element.41.refs_3_), channel_id=1, source_target_pairs={{0,8},{1,9},{2,10},{3,11},{4,5},{5,4},{6,7},{7,6},{8,0},{9,1},{10,... | collective-permute-start | bytes 1179656 | tf_op jit(solution)/shard_map/ppermute | solution.py:348
  79.5 46.0 %collective-permute-start.14 = (bf16[3,512,128]{2,1,0:T(8,128)(2,1)}, bf16[3,512,128]{2,1,0:T(8,128)(2,1)S(1)}, u32[]{:S(2)}, u32[]{:S(2)}) collective-permute-start(bf16[3,512,128]{2,1,0:T(8,128)(2,1)} %get-tuple-element.41.refs_3_), channel_id=1, source_target_pairs={{0,8},{1,9},{2,10},{3,11},{4,6},{5,7},{6,4},{7,5},{8,0},{9,1},{10,... | collective-permute-start | bytes 1179656 | tf_op jit(solution)/shard_map/ppermute | solution.py:348
  82.4 43.2 %collective-permute-start.15 = (bf16[3,512,128]{2,1,0:T(8,128)(2,1)}, bf16[3,512,128]{2,1,0:T(8,128)(2,1)S(1)}, u32[]{:S(2)}, u32[]{:S(2)}) collective-permute-start(bf16[3,512,128]{2,1,0:T(8,128)(2,1)} %get-tuple-element.41.refs_3_), channel_id=1, source_target_pairs={{0,8},{1,9},{2,10},{3,11},{4,7},{5,6},{6,5},{7,4},{8,0},{9,1},{10,... | collective-permute-start | bytes 1179656 | tf_op jit(solution)/shard_map/ppermute | solution.py:348
  86.5 118.9 %collective-permute-start.5 = (bf16[2,512,768]{2,1,0:T(8,128)(2,1)}, bf16[2,512,768]{2,1,0:T(8,128)(2,1)S(1)}, u32[]{:S(2)}, u32[]{:S(2)}) collective-permute-start(bf16[2,512,768]{2,1,0:T(8,128)(2,1)} %get-tuple-element.35), channel_id=1, source_target_pairs={{3,4},{4,5},{5,6},{6,7},{11,12},{12,13},{13,14},{14,15},{19,20},{2... | collective-permute-start | bytes 4718600 | tf_op jit(solution)/shard_map/ppermute | solution.py:348
  88.4 119.5 %collective-permute-start.3 = (bf16[2,512,768]{2,1,0:T(8,128)(2,1)}, bf16[2,512,768]{2,1,0:T(8,128)(2,1)}, u32[]{:S(2)}, u32[]{:S(2)}) collective-permute-start(bf16[2,512,768]{2,1,0:T(8,128)(2,1)} %get-tuple-element.35), channel_id=1, source_target_pairs={{0,1},{1,2},{2,3},{8,9},{9,10},{10,11},{16,17},{17,18},{18,19},{24... | collective-permute-start | bytes 4718600 | tf_op jit(solution)/shard_map/ppermute | solution.py:348
  125.5 18.6 %collective-permute-start.20 = (bf16[3,512,128]{2,1,0:T(8,128)(2,1)}, bf16[3,512,128]{2,1,0:T(8,128)(2,1)}, u32[]{:S(2)}, u32[]{:S(2)}) collective-permute-start(bf16[3,512,128]{2,1,0:T(8,128)(2,1)} %get-tuple-element.47.refs_3_), channel_id=1, source_target_pairs={{0,8},{1,9},{2,10},{3,11},{4,5},{5,4},{6,7},{7,6},{8,0},{9,1},{10,... | collective-permute-start | bytes 1179656 | tf_op jit(solution)/shard_map/ppermute | solution.py:348
  125.5 21.1 %collective-permute-start.21 = (bf16[3,512,128]{2,1,0:T(8,128)(2,1)}, bf16[3,512,128]{2,1,0:T(8,128)(2,1)}, u32[]{:S(2)}, u32[]{:S(2)}) collective-permute-start(bf16[3,512,128]{2,1,0:T(8,128)(2,1)} %get-tuple-element.47.refs_3_), channel_id=1, source_target_pairs={{0,8},{1,9},{2,10},{3,11},{4,6},{5,7},{6,4},{7,5},{8,0},{9,1},{10,... | collective-permute-start | bytes 1179656 | tf_op jit(solution)/shard_map/ppermute | solution.py:348
  125.6 21.4 %collective-permute-start.22 = (bf16[3,512,128]{2,1,0:T(8,128)(2,1)}, bf16[3,512,128]{2,1,0:T(8,128)(2,1)}, u32[]{:S(2)}, u32[]{:S(2)}) collective-permute-start(bf16[3,512,128]{2,1,0:T(8,128)(2,1)} %get-tuple-element.47.refs_3_), channel_id=1, source_target_pairs={{0,8},{1,9},{2,10},{3,11},{4,7},{5,6},{6,5},{7,4},{8,0},{9,1},{10,... | collective-permute-start | bytes 1179656 | tf_op jit(solution)/shard_map/ppermute | solution.py:348
  147.0 19.3 %collective-permute-start.18 = (bf16[3,512,128]{2,1,0:T(8,128)(2,1)}, bf16[3,512,128]{2,1,0:T(8,128)(2,1)S(1)}, u32[]{:S(2)}, u32[]{:S(2)}) collective-permute-start(bf16[3,512,128]{2,1,0:T(8,128)(2,1)} %get-tuple-element.45), channel_id=1, source_target_pairs={{0,8},{1,9},{2,10},{3,11},{4,7},{5,6},{6,5},{7,4},{8,0},{9,1},{10,... | collective-permute-start | bytes 1179656 | tf_op jit(solution)/shard_map/ppermute | solution.py:348
  159.6 20.7 %collective-permute-start.23 = (bf16[3,512,128]{2,1,0:T(8,128)(2,1)}, bf16[3,512,128]{2,1,0:T(8,128)(2,1)S(1)}, u32[]{:S(2)}, u32[]{:S(2)}) collective-permute-start(bf16[3,512,128]{2,1,0:T(8,128)(2,1)} %get-tuple-element.49), channel_id=1, source_target_pairs={{0,8},{1,9},{2,10},{3,11},{4,5},{5,4},{6,7},{7,6},{8,0},{9,1},{10,... | collective-permute-start | bytes 1179656 | tf_op jit(solution)/shard_map/ppermute | solution.py:348
  161.6 29.0 %collective-permute-start.24 = (bf16[3,512,128]{2,1,0:T(8,128)(2,1)}, bf16[3,512,128]{2,1,0:T(8,128)(2,1)S(1)}, u32[]{:S(2)}, u32[]{:S(2)}) collective-permute-start(bf16[3,512,128]{2,1,0:T(8,128)(2,1)} %get-tuple-element.50), channel_id=1, source_target_pairs={{0,8},{1,9},{2,10},{3,11},{4,6},{5,7},{6,4},{7,5},{8,0},{9,1},{10,... | collective-permute-start | bytes 1179656 | tf_op jit(solution)/shard_map/ppermute | solution.py:348
  167.1 24.0 %collective-permute-start.25 = (bf16[3,512,128]{2,1,0:T(8,128)(2,1)}, bf16[3,512,128]{2,1,0:T(8,128)(2,1)S(1)}, u32[]{:S(2)}, u32[]{:S(2)}) collective-permute-start(bf16[3,512,128]{2,1,0:T(8,128)(2,1)} %get-tuple-element.51), channel_id=1, source_target_pairs={{0,8},{1,9},{2,10},{3,11},{4,7},{5,6},{6,5},{7,4},{8,0},{9,1},{10,... | collective-permute-start | bytes 1179656 | tf_op jit(solution)/shard_map/ppermute | solution.py:348
  180.3 26.5 %collective-permute-start.29 = (bf16[3,512,128]{2,1,0:T(8,128)(2,1)}, bf16[3,512,128]{2,1,0:T(8,128)(2,1)S(1)}, u32[]{:S(2)}, u32[]{:S(2)}) collective-permute-start(bf16[3,512,128]{2,1,0:T(8,128)(2,1)} %shard_map.80._.refs_3_), channel_id=1, source_target_pairs={{0,1},{1,0},{2,3},{3,2},{4,5},{5,4},{6,7},{7,6},{8,9},{9,8},{10,11... | collective-permute-start | bytes 1179656 | tf_op jit(solution)/shard_map/ppermute | solution.py:348
  190.7 34.2 %collective-permute-start.30 = (bf16[3,512,128]{2,1,0:T(8,128)(2,1)}, bf16[3,512,128]{2,1,0:T(8,128)(2,1)}, u32[]{:S(2)}, u32[]{:S(2)}) collective-permute-start(bf16[3,512,128]{2,1,0:T(8,128)(2,1)} %shard_map.80._.refs_3_), channel_id=1, source_target_pairs={{0,2},{1,3},{2,0},{3,1},{4,6},{5,7},{6,4},{7,5},{8,10},{9,11},{10,... | collective-permute-start | bytes 1179656 | tf_op jit(solution)/shard_map/ppermute | solution.py:348
  191.1 33.8 %collective-permute-start.31 = (bf16[3,512,128]{2,1,0:T(8,128)(2,1)}, bf16[3,512,128]{2,1,0:T(8,128)(2,1)}, u32[]{:S(2)}, u32[]{:S(2)}) collective-permute-start(bf16[3,512,128]{2,1,0:T(8,128)(2,1)} %shard_map.80._.refs_3_), channel_id=1, source_target_pairs={{0,3},{1,2},{2,1},{3,0},{4,7},{5,6},{6,5},{7,4},{8,11},{9,10},{10,... | collective-permute-start | bytes 1179656 | tf_op jit(solution)/shard_map/ppermute | solution.py:348
  205.3 29.7 %collective-permute-start.26 = (bf16[3,512,128]{2,1,0:T(8,128)(2,1)}, bf16[3,512,128]{2,1,0:T(8,128)(2,1)}, u32[]{:S(2)}, u32[]{:S(2)}) collective-permute-start(bf16[3,512,128]{2,1,0:T(8,128)(2,1)} %shard_map.84.refs_3_), channel_id=1, source_target_pairs={{0,1},{1,0},{2,3},{3,2},{4,5},{5,4},{6,7},{7,6},{8,9},{9,8},{10,11... | collective-permute-start | bytes 1179656 | tf_op jit(solution)/shard_map/ppermute | solution.py:348
  207.5 27.5 %collective-permute-start.27 = (bf16[3,512,128]{2,1,0:T(8,128)(2,1)}, bf16[3,512,128]{2,1,0:T(8,128)(2,1)}, u32[]{:S(2)}, u32[]{:S(2)}) collective-permute-start(bf16[3,512,128]{2,1,0:T(8,128)(2,1)} %shard_map.84.refs_3_), channel_id=1, source_target_pairs={{0,2},{1,3},{2,0},{3,1},{4,6},{5,7},{6,4},{7,5},{8,10},{9,11},{10,... | collective-permute-start | bytes 1179656 | tf_op jit(solution)/shard_map/ppermute | solution.py:348
  207.9 27.1 %collective-permute-start.28 = (bf16[3,512,128]{2,1,0:T(8,128)(2,1)}, bf16[3,512,128]{2,1,0:T(8,128)(2,1)}, u32[]{:S(2)}, u32[]{:S(2)}) collective-permute-start(bf16[3,512,128]{2,1,0:T(8,128)(2,1)} %shard_map.84.refs_3_), channel_id=1, source_target_pairs={{0,3},{1,2},{2,1},{3,0},{4,7},{5,6},{6,5},{7,4},{8,11},{9,10},{10,... | collective-permute-start | bytes 1179656 | tf_op jit(solution)/shard_map/ppermute | solution.py:348
  (34 other events, 351.7 us)

commit v2 on v1

--- a/solution.py
+++ b/solution.py
@@ -348,21 +348,20 @@
     return lax.ppermute(x, axes, route)
 
 
+def trade(x, partner):
+    rows, cols = lax.axis_size("head"), lax.axis_size("seq")
+    route = []
+    for h in range(rows):
+        for i in range(cols):
+            if i in partner:
+                route.append((h * cols + i, h * cols + partner[i]))
+            elif rows % 2 == 0:
+                route.append((h * cols + i, (h ^ 1) * cols + i))
+    return hop(x, route, ("head", "seq"))
+
+
 def spread(xs, low, high):
-    rows, cols = lax.axis_size("head"), lax.axis_size("seq")
-    got = []
-    for d, x in enumerate(xs):
-        if d == 0:
-            continue
-        route = []
-        for h in range(rows):
-            for i in range(cols):
-                if low <= i < high:
-                    route.append((h * cols + i, h * cols + (i ^ d)))
-                elif rows % 2 == 0:
-                    route.append((h * cols + i, (h ^ 1) * cols + i))
-        got.append(hop(x, route, ("head", "seq")))
-    return got
+    return [trade(x, {i: i ^ d for i in range(low, high)}) for d, x in enumerate(xs) if d]
 
 
 def fast_device(queries, key_rows, value_rows, learn_rates, gate_fast, down_fast, up_fast):
@@ -381,10 +380,10 @@
 
     count = queries.shape[1] // AH
     main, rest = tail_rows(key_rows, value_rows, (count - count // 4) * AH)
-    side_a = hop(rest, [(parts - 1, parts - 2)])
+    side_a = trade(rest, {parts - 1: parts - 2, parts - 2: parts - 1})
     main_a = hop(main, early)
     rest_a = hop(rest, early[1:])
-    relay_a = hop(side_a, [(parts - 2, parts)])
+    relay_a = trade(side_a, {parts - 2: parts, parts: parts - 2})
     terms = [grads(pos, h, parts, key_rows, value_rows, rates, first_w, True) for h in span]
 
     def attend_inner(h, after):

time: 243 us -> 243 us (level)
  starting transfers between devices: 33.5 us -> 30.8 us
  waiting for transfers between devices: 89.9 us -> 92.6 us
    ppermute x32, waiting for transfers between devices: 89.9 us -> 92.6 us  [hop(): return lax.ppermute(x, axes, route)]
    ppermute x32, starting transfers between devices: 33.5 us -> 30.8 us  [hop(): return lax.ppermute(x, axes, route)]
where the time goes in v2:
time: 243 us; the launch traced here: 242 us
  Pallas kernels  109 us (45%)
  waiting for transfers between devices  92.6 us (38%)
  starting transfers between devices  30.8 us (13%)
  local copies, waits for them, and re-layouts  6.56 us (3%)
    ppermute x32, waiting for transfers between devices, hop(): return lax.ppermute(x, axes, route)  92.6 us
    pallas_call x4, Pallas kernels, grads(): pl.pallas_call(functools.partial(grads_kernel, parts, whole, head), out_s...  46.6 us
    ppermute x32, starting transfers between devices, hop(): return lax.ppermute(x, axes, route)  30.8 us
    pallas_call x2, Pallas kernels, inner_attention(): pl.pallas_call(inner_kernel, out_shape=jax.ShapeDtypeStruct((rows - WINDO...  18 us
    pallas_call x2, Pallas kernels, edge_attention(): pl.pallas_call(functools.partial(edge_kernel, side, kept), out_shape=jax....  15.3 us
    pallas_call x2, Pallas kernels, apply_fast(): pl.pallas_call(functools.partial(apply_kernel, parts), out_shape=jax.Shap...  13.2 us
    pallas_call x2, Pallas kernels, renew_second(): pl.pallas_call(renew_second_kernel, out_shape=jax.ShapeDtypeStruct(weight...  6.96 us
    pallas_call x2, Pallas kernels, renew_first(): pl.pallas_call(renew_first_kernel, out_shape=[jax.ShapeDtypeStruct(own.sh...  6.73 us
  transfers between devices with their start and end apart: 32, of which 7 were waited for; matrix products, arithmetic and copies ran while one was open for 1% of the time, Pallas kernels for 38%

profile of v2, /device:TPU:26, one launch (start us, length us, event | category | flops | bytes accessed | tf_op | source)
XLA Modules:
  0.0 241.6 jit_solution(5247674872450763901)
XLA Ops:
  0.6 11.8 %shard_map.77 = (bf16[3,512,128]{2,1,0:T(8,128)(2,1)}, bf16[3,512,128]{2,1,0:T(8,128)(2,1)}, bf16[3,512,128]{2,1,0:T(8,128)(2,1)}, bf16[3,512,128]{2,1,0:T(8,128)(2,1)}) custom-call(s32[3]{0:T(128)} %pad_add_fusion.pos_ref, bf16[1536,1024]{1,0:T(8,128)(2,1)} %k_ref.9, bf16[1536,1024]{1,0:T(8,128)(2,1)} %v_ref.9, bf16[2,1536]{1,0:T(2,128)(2,1)} %bitcast.4, ...), custom_call_target="tpu_custom_call" | custom-call | flops 4831838208 | bytes 6291456 | tf_op jit(solution)/shard_map/pallas_call | solution.py:93
  12.9 11.7 %shard_map.74 = (bf16[3,512,128]{2,1,0:T(8,128)(2,1)}, bf16[3,512,128]{2,1,0:T(8,128)(2,1)}, bf16[3,512,128]{2,1,0:T(8,128)(2,1)}, bf16[3,512,128]{2,1,0:T(8,128)(2,1)}) custom-call(s32[3]{0:T(128)} %pad_add_fusion.pos_ref, bf16[1536,1024]{1,0:T(8,128)(2,1)} %k_ref.9, bf16[1536,1024]{1,0:T(8,128)(2,1)} %v_ref.9, bf16[2,1536]{1,0:T(2,128)(2,1)} %bitcast.5, ...), custom_call_target="tpu_custom_call" | custom-call | flops 4831838208 | bytes 6291456 | tf_op jit(solution)/shard_map/pallas_call | solution.py:93
  25.7 2.6 %shard_map.73 = (bf16[2,512,768]{2,1,0:T(8,128)(2,1)}, bf16[2,512,256]{2,1,0:T(8,128)(2,1)}) custom-call(bf16[1536,1024]{1,0:T(8,128)(2,1)} %k_ref.9, bf16[1536,1024]{1,0:T(8,128)(2,1)} %v_ref.9), custom_call_target="tpu_custom_call" | custom-call | bytes 4194304 | tf_op jit(solution)/shard_map/pallas_call | solution.py:124
  28.5 3.4 %collective-permute-start.6 = (bf16[2,512,256]{2,1,0:T(8,128)(2,1)}, bf16[2,512,256]{2,1,0:T(8,128)(2,1)S(1)}, u32[]{:S(2)}, u32[]{:S(2)}) collective-permute-start(bf16[2,512,256]{2,1,0:T(8,128)(2,1)} %get-tuple-element.36), channel_id=1, source_target_pairs={{4,5},{5,6},{6,7},{12,13},{13,14},{14,15},{20,21},{21,22},{22,23},... | collective-permute-start | bytes 1572872 | tf_op jit(solution)/shard_map/ppermute | solution.py:348
  36.9 37.1 %collective-permute-done.12.far_ref = bf16[3,512,128]{2,1,0:T(8,128)(2,1)S(1)} collective-permute-done((bf16[3,512,128]{2,1,0:T(8,128)(2,1)S(1)}, bf16[3,512,128]{2,1,0:T(8,128)(2,1)S(1)}, u32[]{:S(2)}, u32[]{:S(2)}) %collective-permute-start.12) | collective-permute-done | bytes 393248 | tf_op jit(solution)/shard_map/ppermute | solution.py:348
  74.7 3.4 %shard_map.78 = (f32[3,512,128]{2,1,0:T(8,128)}, bf16[3,512,128]{2,1,0:T(8,128)(2,1)}) custom-call(s32[3]{0:T(128)} %pad_add_fusion.pos_ref, bf16[3,512,128]{2,1,0:T(8,128)(2,1)} %copy-done.8, bf16[3,512,128]{2,1,0:T(8,128)(2,1)} %copy-done.14, f32[2,512,512]{2,1,0:T(8,128)} %g_ref.3, f32[2,512,512]{2,1,0:T(8,128)} %u_ref.3, f32[2,512,512]{2,1,0:T(8,128)} %d_ref.3), custom_call_target="tpu_custom_call" | custom-call | flops 1179648 | bytes 2621440 | tf_op jit(solution)/shard_map/pallas_call | solution.py:154
  79.5 2.9 %collective-permute-done.19.far_ref = bf16[3,512,128]{2,1,0:T(8,128)(2,1)S(1)} collective-permute-done((bf16[3,512,128]{2,1,0:T(8,128)(2,1)S(1)}, bf16[3,512,128]{2,1,0:T(8,128)(2,1)S(1)}, u32[]{:S(2)}, u32[]{:S(2)}) %collective-permute-start.19) | collective-permute-done | bytes 393248 | tf_op jit(solution)/shard_map/ppermute | solution.py:348
  83.1 3.4 %shard_map.82 = (f32[3,512,128]{2,1,0:T(8,128)}, bf16[3,512,128]{2,1,0:T(8,128)(2,1)}) custom-call(s32[3]{0:T(128)} %pad_add_fusion.pos_ref, bf16[3,512,128]{2,1,0:T(8,128)(2,1)} %copy-done.10, bf16[3,512,128]{2,1,0:T(8,128)(2,1)} %copy-done.13, f32[2,512,512]{2,1,0:T(8,128)} %g_ref.3, f32[2,512,512]{2,1,0:T(8,128)} %u_ref.3, f32[2,512,512]{2,1,0:T(8,128)} %d_ref.3), custom_call_target="tpu_custom_call" | custom-call | flops 1179648 | bytes 2621440 | tf_op jit(solution)/shard_map/pallas_call | solution.py:154
  90.2 35.3 %collective-permute-done.13.refs_4_ = bf16[3,512,128]{2,1,0:T(8,128)(2,1)S(1)} collective-permute-done((bf16[3,512,128]{2,1,0:T(8,128)(2,1)}, bf16[3,512,128]{2,1,0:T(8,128)(2,1)S(1)}, u32[]{:S(2)}, u32[]{:S(2)}) %collective-permute-start.13) | collective-permute-done | bytes 393248 | tf_op jit(solution)/shard_map/ppermute | solution.py:348
  125.6 3.4 %collective-permute-start.22 = (bf16[3,512,128]{2,1,0:T(8,128)(2,1)}, bf16[3,512,128]{2,1,0:T(8,128)(2,1)}, u32[]{:S(2)}, u32[]{:S(2)}) collective-permute-start(bf16[3,512,128]{2,1,0:T(8,128)(2,1)} %get-tuple-element.47.refs_3_), channel_id=1, source_target_pairs={{0,8},{1,9},{2,10},{3,11},{4,7},{5,6},{6,5},{7,4},{8,0},{9,1},{10,... | collective-permute-start | bytes 1179656 | tf_op jit(solution)/shard_map/ppermute | solution.py:348
  129.0 11.6 %shard_map.79 = (bf16[3,512,128]{2,1,0:T(8,128)(2,1)}, bf16[3,512,128]{2,1,0:T(8,128)(2,1)}, bf16[3,512,128]{2,1,0:T(8,128)(2,1)}, bf16[3,512,128]{2,1,0:T(8,128)(2,1)}) custom-call(s32[3]{0:T(128)} %pad_add_fusion.pos_ref, bf16[1536,1024]{1,0:T(8,128)(2,1)} %k_ref.9, bf16[1536,1024]{1,0:T(8,128)(2,1)} %v_ref.9, bf16[2,1536]{1,0:T(2,128)(2,1)} %bitcast.6, ...), custom_call_target="tpu_custom_call" | custom-call | flops 4831838208 | bytes 6291456 | tf_op jit(solution)/shard_map/pallas_call | solution.py:93
  140.6 3.5 %collective-permute-done.20.refs_4_ = bf16[3,512,128]{2,1,0:T(8,128)(2,1)} collective-permute-done((bf16[3,512,128]{2,1,0:T(8,128)(2,1)}, bf16[3,512,128]{2,1,0:T(8,128)(2,1)}, u32[]{:S(2)}, u32[]{:S(2)}) %collective-permute-start.20) | collective-permute-done | bytes 393248 | tf_op jit(solution)/shard_map/ppermute | solution.py:348
  144.1 2.5 %collective-permute-start.16 = (bf16[3,512,128]{2,1,0:T(8,128)(2,1)}, bf16[3,512,128]{2,1,0:T(8,128)(2,1)S(1)}, u32[]{:S(2)}, u32[]{:S(2)}) collective-permute-start(bf16[3,512,128]{2,1,0:T(8,128)(2,1)} %get-tuple-element.43), channel_id=1, source_target_pairs={{0,8},{1,9},{2,10},{3,11},{4,5},{5,4},{6,7},{7,6},{8,0},{9,1},{10,... | collective-permute-start | bytes 1179656 | tf_op jit(solution)/shard_map/ppermute | solution.py:348
  148.1 11.5 %shard_map.83 = (bf16[3,512,128]{2,1,0:T(8,128)(2,1)}, bf16[3,512,128]{2,1,0:T(8,128)(2,1)}, bf16[3,512,128]{2,1,0:T(8,128)(2,1)}, bf16[3,512,128]{2,1,0:T(8,128)(2,1)}) custom-call(s32[3]{0:T(128)} %pad_add_fusion.pos_ref, bf16[1536,1024]{1,0:T(8,128)(2,1)} %k_ref.9, bf16[1536,1024]{1,0:T(8,128)(2,1)} %v_ref.9, bf16[2,1536]{1,0:T(2,128)(2,1)} %bitcast.7, ...), custom_call_target="tpu_custom_call" | custom-call | flops 4831838208 | bytes 6291456 | tf_op jit(solution)/shard_map/pallas_call | solution.py:93
  162.1 4.2 %collective-permute-done.18.refs_3_ = bf16[3,512,128]{2,1,0:T(8,128)(2,1)S(1)} collective-permute-done((bf16[3,512,128]{2,1,0:T(8,128)(2,1)}, bf16[3,512,128]{2,1,0:T(8,128)(2,1)S(1)}, u32[]{:S(2)}, u32[]{:S(2)}) %collective-permute-start.18) | collective-permute-done | bytes 393248 | tf_op jit(solution)/shard_map/ppermute | solution.py:348
  167.6 3.5 %shard_map.80._.refs_3_ = bf16[3,512,128]{2,1,0:T(8,128)(2,1)} custom-call(s32[3]{0:T(128)} %pad_add_fusion.pos_ref, bf16[3,512,128]{2,1,0:T(8,128)(2,1)} %get-tuple-element.42.refs_0_, bf16[3,512,128]{2,1,0:T(8,128)(2,1)} %copy-done.18, bf16[3,512,128]{2,1,0:T(8,128)(2,1)} %copy-done.20, bf16[3,512,128]{2,1,0:T(8,128)(2,1)} %copy-done.22, ...), custom_call_target="tpu_custom_call" | custom-call | flops 1572864 | bytes 2621440 | tf_op jit(solution)/shard_map/pallas_call | solution.py:181
  171.1 9.2 %collective-permute-done.23.refs_1_ = bf16[3,512,128]{2,1,0:T(8,128)(2,1)S(1)} collective-permute-done((bf16[3,512,128]{2,1,0:T(8,128)(2,1)}, bf16[3,512,128]{2,1,0:T(8,128)(2,1)S(1)}, u32[]{:S(2)}, u32[]{:S(2)}) %collective-permute-start.23) | collective-permute-done | bytes 393248 | tf_op jit(solution)/shard_map/ppermute | solution.py:348
  181.7 9.0 %shard_map.85.refs_2_ = bf16[1024,512]{1,0:T(8,128)(2,1)} custom-call(bf16[1536,1024]{1,0:T(8,128)(2,1)} %refs_0_.11, bf16[1536,1024]{1,0:T(8,128)(2,1)} %k_ref.9, bf16[1536,1024]{1,0:T(8,128)(2,1)} %v_ref.9, bf16[3,512,128]{2,1,0:T(8,128)(2,1)} %copy-done.8), custom_call_target="tpu_custom_call" | custom-call | flops 2415919104 | bytes 7864320 | tf_op jit(solution)/shard_map/pallas_call | solution.py:221
  192.8 9.0 %shard_map.81.refs_2_ = bf16[1024,512]{1,0:T(8,128)(2,1)} custom-call(bf16[1536,1024]{1,0:T(8,128)(2,1)} %refs_0_.11, bf16[1536,1024]{1,0:T(8,128)(2,1)} %k_ref.9, bf16[1536,1024]{1,0:T(8,128)(2,1)} %v_ref.9, bf16[3,512,128]{2,1,0:T(8,128)(2,1)} %shard_map.80._.refs_3_), custom_call_target="tpu_custom_call" | custom-call | flops 2415919104 | bytes 7864320 | tf_op jit(solution)/shard_map/pallas_call | solution.py:221
  201.9 3.5 %shard_map.84.refs_3_ = bf16[3,512,128]{2,1,0:T(8,128)(2,1)} custom-call(s32[3]{0:T(128)} %pad_add_fusion.pos_ref, bf16[3,512,128]{2,1,0:T(8,128)(2,1)} %get-tuple-element.48.refs_0_, bf16[3,512,128]{2,1,0:T(8,128)(2,1)} %copy-done.16, bf16[3,512,128]{2,1,0:T(8,128)(2,1)} %copy-done.19, bf16[3,512,128]{2,1,0:T(8,128)(2,1)} %copy-done.21, ...), custom_call_target="tpu_custom_call" | custom-call | flops 1572864 | bytes 2621440 | tf_op jit(solution)/shard_map/pallas_call | solution.py:181
  209.6 11.4 %shard_map.75.refs_0_ = bf16[512,1024]{1,0:T(8,128)(2,1)} custom-call(s32[3]{0:T(128)} %pad_add_fusion.pos_ref, bf16[1536,1024]{1,0:T(8,128)(2,1)} %refs_0_.11, bf16[1536,1024]{1,0:T(8,128)(2,1)} %k_ref.9, bf16[1536,1024]{1,0:T(8,128)(2,1)} %v_ref.9, bf16[2,512,768]{2,1,0:T(8,128)(2,1)} %copy-done.11, bf16[2,512,256]{2,1,0:T(8,128)(2,1)} %copy-done.12, ...), custom_call_target="tpu_custom_call" | custom-call | flops 1610612736 | bytes 9437184 | tf_op jit(solution)/shard_map/pallas_call | solution.py:269
  221.0 3.9 %shard_map.76.refs_1_ = bf16[512,1024]{1,0:T(8,128)(2,1)} custom-call(s32[3]{0:T(128)} %pad_add_fusion.pos_ref, bf16[1536,1024]{1,0:T(8,128)(2,1)} %refs_0_.11, bf16[1536,1024]{1,0:T(8,128)(2,1)} %k_ref.9, bf16[1536,1024]{1,0:T(8,128)(2,1)} %v_ref.9, bf16[2,512,768]{2,1,0:T(8,128)(2,1)} %collective-permute-done.3.main_ref, ...), custom_call_target="tpu_custom_call", output_to_operand_aliasing={{}: (7, {})} | custom-call | flops 1610612736 | bytes 9437184 | tf_op jit(solution)/shard_map/pallas_call | solution.py:269
  228.4 6.6 %shard_map.86.refs_7_ = bf16[1536,1024]{1,0:T(8,128)(2,1)} custom-call(s32[3]{0:T(128)S(1)} %copy-done.7, bf16[1536,1024]{1,0:T(8,128)(2,1)S(1)} %copy-done, bf16[512,1024]{1,0:T(8,128)(2,1)S(1)} %copy-done.1, bf16[1024,512]{1,0:T(8,128)(2,1)S(1)} %copy-done.2, bf16[3,512,128]{2,1,0:T(8,128)(2,1)} %shard_map.80._.refs_3_, ...), custom_call_target="tpu_custom_call" | custom-call | flops 2415919104 | bytes 7864320 | tf_op jit(solution)/shard_map/pallas_call | solution.py:329
  235.0 6.6 %shard_map.87 = bf16[1536,1024]{1,0:T(8,128)(2,1)} custom-call(s32[3]{0:T(128)S(1)} %copy-done.7, bf16[1536,1024]{1,0:T(8,128)(2,1)S(1)} %copy-done, bf16[512,1024]{1,0:T(8,128)(2,1)S(1)} %copy-done.1, bf16[1024,512]{1,0:T(8,128)(2,1)S(1)} %copy-done.3, bf16[3,512,128]{2,1,0:T(8,128)(2,1)S(1)} %copy-done.4, ...), custom_call_target="tpu_custom_call", output_to_operand_aliasing={{}: (8, {})} | custom-call | flops 2415919104 | bytes 7864320 | tf_op jit(solution)/shard_map/pallas_call | solution.py:329
  (110 shorter events, 30.6 us)
Async XLA Ops:
  12.4 15.9 %collective-permute-start.11 = (bf16[3,512,128]{2,1,0:T(8,128)(2,1)}, bf16[3,512,128]{2,1,0:T(8,128)(2,1)S(1)}, u32[]{:S(2)}, u32[]{:S(2)}) collective-permute-start(bf16[3,512,128]{2,1,0:T(8,128)(2,1)} %get-tuple-element.40), channel_id=1, source_target_pairs={{0,3},{1,2},{2,1},{3,0},{4,12},{5,13},{6,14},{7,15},{8,11},{9,10},... | collective-permute-start | bytes 1179656 | tf_op jit(solution)/shard_map/ppermute | solution.py:348
  28.5 51.0 %collective-permute-start.6 = (bf16[2,512,256]{2,1,0:T(8,128)(2,1)}, bf16[2,512,256]{2,1,0:T(8,128)(2,1)S(1)}, u32[]{:S(2)}, u32[]{:S(2)}) collective-permute-start(bf16[2,512,256]{2,1,0:T(8,128)(2,1)} %get-tuple-element.36), channel_id=1, source_target_pairs={{4,5},{5,6},{6,7},{12,13},{13,14},{14,15},{20,21},{21,22},{22,23},... | collective-permute-start | bytes 1572872 | tf_op jit(solution)/shard_map/ppermute | solution.py:348
  32.2 41.8 %collective-permute-start.12 = (bf16[3,512,128]{2,1,0:T(8,128)(2,1)S(1)}, bf16[3,512,128]{2,1,0:T(8,128)(2,1)S(1)}, u32[]{:S(2)}, u32[]{:S(2)}) collective-permute-start(bf16[3,512,128]{2,1,0:T(8,128)(2,1)S(1)} %add_convert_fusion.own_ref._), channel_id=1, source_target_pairs={{0,4},{1,5},{2,6},{3,7},{8,12},{9,13},{10,14},{11,15},{16,20},{17,... | collective-permute-start | bytes 1179656 | tf_op jit(solution)/shard_map/ppermute | solution.py:348
  34.7 47.7 %collective-permute-start.19 = (bf16[3,512,128]{2,1,0:T(8,128)(2,1)S(1)}, bf16[3,512,128]{2,1,0:T(8,128)(2,1)S(1)}, u32[]{:S(2)}, u32[]{:S(2)}) collective-permute-start(bf16[3,512,128]{2,1,0:T(8,128)(2,1)S(1)} %add_convert_fusion.1.own_ref), channel_id=1, source_target_pairs={{0,4},{1,5},{2,6},{3,7},{8,12},{9,13},{10,14},{11,15},{16,20},{17,... | collective-permute-start | bytes 1179656 | tf_op jit(solution)/shard_map/ppermute | solution.py:348
  36.0 50.5 %collective-permute-start.4 = (bf16[2,512,256]{2,1,0:T(8,128)(2,1)}, bf16[2,512,256]{2,1,0:T(8,128)(2,1)S(1)}, u32[]{:S(2)}, u32[]{:S(2)}) collective-permute-start(bf16[2,512,256]{2,1,0:T(8,128)(2,1)} %get-tuple-element.36), channel_id=1, source_target_pairs={{0,1},{1,2},{2,3},{8,9},{9,10},{10,11},{16,17},{17,18},{18,19},{24... | collective-permute-start | bytes 1572872 | tf_op jit(solution)/shard_map/ppermute | solution.py:348
  36.7 51.7 %collective-permute-start.8 = (bf16[2,512,256]{2,1,0:T(8,128)(2,1)}, bf16[2,512,256]{2,1,0:T(8,128)(2,1)}, u32[]{:S(2)}, u32[]{:S(2)}) collective-permute-start(bf16[2,512,256]{2,1,0:T(8,128)(2,1)} %collective-permute-done.7), channel_id=1, source_target_pairs={{0,8},{1,9},{2,4},{3,11},{4,2},{5,13},{6,14},{7,15},{8,0},{9,1},{1... | collective-permute-start | bytes 1572872 | tf_op jit(solution)/shard_map/ppermute | solution.py:348
  78.1 47.4 %collective-permute-start.13 = (bf16[3,512,128]{2,1,0:T(8,128)(2,1)}, bf16[3,512,128]{2,1,0:T(8,128)(2,1)S(1)}, u32[]{:S(2)}, u32[]{:S(2)}) collective-permute-start(bf16[3,512,128]{2,1,0:T(8,128)(2,1)} %get-tuple-element.41.refs_3_), channel_id=1, source_target_pairs={{0,8},{1,9},{2,10},{3,11},{4,5},{5,4},{6,7},{7,6},{8,0},{9,1},{10,... | collective-permute-start | bytes 1179656 | tf_op jit(solution)/shard_map/ppermute | solution.py:348
  79.5 46.0 %collective-permute-start.14 = (bf16[3,512,128]{2,1,0:T(8,128)(2,1)}, bf16[3,512,128]{2,1,0:T(8,128)(2,1)S(1)}, u32[]{:S(2)}, u32[]{:S(2)}) collective-permute-start(bf16[3,512,128]{2,1,0:T(8,128)(2,1)} %get-tuple-element.41.refs_3_), channel_id=1, source_target_pairs={{0,8},{1,9},{2,10},{3,11},{4,6},{5,7},{6,4},{7,5},{8,0},{9,1},{10,... | collective-permute-start | bytes 1179656 | tf_op jit(solution)/shard_map/ppermute | solution.py:348
  82.4 43.2 %collective-permute-start.15 = (bf16[3,512,128]{2,1,0:T(8,128)(2,1)}, bf16[3,512,128]{2,1,0:T(8,128)(2,1)S(1)}, u32[]{:S(2)}, u32[]{:S(2)}) collective-permute-start(bf16[3,512,128]{2,1,0:T(8,128)(2,1)} %get-tuple-element.41.refs_3_), channel_id=1, source_target_pairs={{0,8},{1,9},{2,10},{3,11},{4,7},{5,6},{6,5},{7,4},{8,0},{9,1},{10,... | collective-permute-start | bytes 1179656 | tf_op jit(solution)/shard_map/ppermute | solution.py:348
  86.5 118.9 %collective-permute-start.5 = (bf16[2,512,768]{2,1,0:T(8,128)(2,1)}, bf16[2,512,768]{2,1,0:T(8,128)(2,1)S(1)}, u32[]{:S(2)}, u32[]{:S(2)}) collective-permute-start(bf16[2,512,768]{2,1,0:T(8,128)(2,1)} %get-tuple-element.35), channel_id=1, source_target_pairs={{3,4},{4,5},{5,6},{6,7},{11,12},{12,13},{13,14},{14,15},{19,20},{2... | collective-permute-start | bytes 4718600 | tf_op jit(solution)/shard_map/ppermute | solution.py:348
  88.4 119.5 %collective-permute-start.3 = (bf16[2,512,768]{2,1,0:T(8,128)(2,1)}, bf16[2,512,768]{2,1,0:T(8,128)(2,1)}, u32[]{:S(2)}, u32[]{:S(2)}) collective-permute-start(bf16[2,512,768]{2,1,0:T(8,128)(2,1)} %get-tuple-element.35), channel_id=1, source_target_pairs={{0,1},{1,2},{2,3},{8,9},{9,10},{10,11},{16,17},{17,18},{18,19},{24... | collective-permute-start | bytes 4718600 | tf_op jit(solution)/shard_map/ppermute | solution.py:348
  125.5 18.6 %collective-permute-start.20 = (bf16[3,512,128]{2,1,0:T(8,128)(2,1)}, bf16[3,512,128]{2,1,0:T(8,128)(2,1)}, u32[]{:S(2)}, u32[]{:S(2)}) collective-permute-start(bf16[3,512,128]{2,1,0:T(8,128)(2,1)} %get-tuple-element.47.refs_3_), channel_id=1, source_target_pairs={{0,8},{1,9},{2,10},{3,11},{4,5},{5,4},{6,7},{7,6},{8,0},{9,1},{10,... | collective-permute-start | bytes 1179656 | tf_op jit(solution)/shard_map/ppermute | solution.py:348
  125.5 21.1 %collective-permute-start.21 = (bf16[3,512,128]{2,1,0:T(8,128)(2,1)}, bf16[3,512,128]{2,1,0:T(8,128)(2,1)}, u32[]{:S(2)}, u32[]{:S(2)}) collective-permute-start(bf16[3,512,128]{2,1,0:T(8,128)(2,1)} %get-tuple-element.47.refs_3_), channel_id=1, source_target_pairs={{0,8},{1,9},{2,10},{3,11},{4,6},{5,7},{6,4},{7,5},{8,0},{9,1},{10,... | collective-permute-start | bytes 1179656 | tf_op jit(solution)/shard_map/ppermute | solution.py:348
  125.6 21.4 %collective-permute-start.22 = (bf16[3,512,128]{2,1,0:T(8,128)(2,1)}, bf16[3,512,128]{2,1,0:T(8,128)(2,1)}, u32[]{:S(2)}, u32[]{:S(2)}) collective-permute-start(bf16[3,512,128]{2,1,0:T(8,128)(2,1)} %get-tuple-element.47.refs_3_), channel_id=1, source_target_pairs={{0,8},{1,9},{2,10},{3,11},{4,7},{5,6},{6,5},{7,4},{8,0},{9,1},{10,... | collective-permute-start | bytes 1179656 | tf_op jit(solution)/shard_map/ppermute | solution.py:348
  147.0 19.3 %collective-permute-start.18 = (bf16[3,512,128]{2,1,0:T(8,128)(2,1)}, bf16[3,512,128]{2,1,0:T(8,128)(2,1)S(1)}, u32[]{:S(2)}, u32[]{:S(2)}) collective-permute-start(bf16[3,512,128]{2,1,0:T(8,128)(2,1)} %get-tuple-element.45), channel_id=1, source_target_pairs={{0,8},{1,9},{2,10},{3,11},{4,7},{5,6},{6,5},{7,4},{8,0},{9,1},{10,... | collective-permute-start | bytes 1179656 | tf_op jit(solution)/shard_map/ppermute | solution.py:348
  159.6 20.7 %collective-permute-start.23 = (bf16[3,512,128]{2,1,0:T(8,128)(2,1)}, bf16[3,512,128]{2,1,0:T(8,128)(2,1)S(1)}, u32[]{:S(2)}, u32[]{:S(2)}) collective-permute-start(bf16[3,512,128]{2,1,0:T(8,128)(2,1)} %get-tuple-element.49), channel_id=1, source_target_pairs={{0,8},{1,9},{2,10},{3,11},{4,5},{5,4},{6,7},{7,6},{8,0},{9,1},{10,... | collective-permute-start | bytes 1179656 | tf_op jit(solution)/shard_map/ppermute | solution.py:348
  161.6 29.0 %collective-permute-start.24 = (bf16[3,512,128]{2,1,0:T(8,128)(2,1)}, bf16[3,512,128]{2,1,0:T(8,128)(2,1)S(1)}, u32[]{:S(2)}, u32[]{:S(2)}) collective-permute-start(bf16[3,512,128]{2,1,0:T(8,128)(2,1)} %get-tuple-element.50), channel_id=1, source_target_pairs={{0,8},{1,9},{2,10},{3,11},{4,6},{5,7},{6,4},{7,5},{8,0},{9,1},{10,... | collective-permute-start | bytes 1179656 | tf_op jit(solution)/shard_map/ppermute | solution.py:348
  167.1 24.0 %collective-permute-start.25 = (bf16[3,512,128]{2,1,0:T(8,128)(2,1)}, bf16[3,512,128]{2,1,0:T(8,128)(2,1)S(1)}, u32[]{:S(2)}, u32[]{:S(2)}) collective-permute-start(bf16[3,512,128]{2,1,0:T(8,128)(2,1)} %get-tuple-element.51), channel_id=1, source_target_pairs={{0,8},{1,9},{2,10},{3,11},{4,7},{5,6},{6,5},{7,4},{8,0},{9,1},{10,... | collective-permute-start | bytes 1179656 | tf_op jit(solution)/shard_map/ppermute | solution.py:348
  180.3 26.5 %collective-permute-start.29 = (bf16[3,512,128]{2,1,0:T(8,128)(2,1)}, bf16[3,512,128]{2,1,0:T(8,128)(2,1)S(1)}, u32[]{:S(2)}, u32[]{:S(2)}) collective-permute-start(bf16[3,512,128]{2,1,0:T(8,128)(2,1)} %shard_map.80._.refs_3_), channel_id=1, source_target_pairs={{0,1},{1,0},{2,3},{3,2},{4,5},{5,4},{6,7},{7,6},{8,9},{9,8},{10,11... | collective-permute-start | bytes 1179656 | tf_op jit(solution)/shard_map/ppermute | solution.py:348
  190.7 34.2 %collective-permute-start.30 = (bf16[3,512,128]{2,1,0:T(8,128)(2,1)}, bf16[3,512,128]{2,1,0:T(8,128)(2,1)}, u32[]{:S(2)}, u32[]{:S(2)}) collective-permute-start(bf16[3,512,128]{2,1,0:T(8,128)(2,1)} %shard_map.80._.refs_3_), channel_id=1, source_target_pairs={{0,2},{1,3},{2,0},{3,1},{4,6},{5,7},{6,4},{7,5},{8,10},{9,11},{10,... | collective-permute-start | bytes 1179656 | tf_op jit(solution)/shard_map/ppermute | solution.py:348
  191.1 33.8 %collective-permute-start.31 = (bf16[3,512,128]{2,1,0:T(8,128)(2,1)}, bf16[3,512,128]{2,1,0:T(8,128)(2,1)}, u32[]{:S(2)}, u32[]{:S(2)}) collective-permute-start(bf16[3,512,128]{2,1,0:T(8,128)(2,1)} %shard_map.80._.refs_3_), channel_id=1, source_target_pairs={{0,3},{1,2},{2,1},{3,0},{4,7},{5,6},{6,5},{7,4},{8,11},{9,10},{10,... | collective-permute-start | bytes 1179656 | tf_op jit(solution)/shard_map/ppermute | solution.py:348
  205.3 29.7 %collective-permute-start.26 = (bf16[3,512,128]{2,1,0:T(8,128)(2,1)}, bf16[3,512,128]{2,1,0:T(8,128)(2,1)}, u32[]{:S(2)}, u32[]{:S(2)}) collective-permute-start(bf16[3,512,128]{2,1,0:T(8,128)(2,1)} %shard_map.84.refs_3_), channel_id=1, source_target_pairs={{0,1},{1,0},{2,3},{3,2},{4,5},{5,4},{6,7},{7,6},{8,9},{9,8},{10,11... | collective-permute-start | bytes 1179656 | tf_op jit(solution)/shard_map/ppermute | solution.py:348
  207.5 27.5 %collective-permute-start.27 = (bf16[3,512,128]{2,1,0:T(8,128)(2,1)}, bf16[3,512,128]{2,1,0:T(8,128)(2,1)}, u32[]{:S(2)}, u32[]{:S(2)}) collective-permute-start(bf16[3,512,128]{2,1,0:T(8,128)(2,1)} %shard_map.84.refs_3_), channel_id=1, source_target_pairs={{0,2},{1,3},{2,0},{3,1},{4,6},{5,7},{6,4},{7,5},{8,10},{9,11},{10,... | collective-permute-start | bytes 1179656 | tf_op jit(solution)/shard_map/ppermute | solution.py:348
  207.9 27.1 %collective-permute-start.28 = (bf16[3,512,128]{2,1,0:T(8,128)(2,1)}, bf16[3,512,128]{2,1,0:T(8,128)(2,1)}, u32[]{:S(2)}, u32[]{:S(2)}) collective-permute-start(bf16[3,512,128]{2,1,0:T(8,128)(2,1)} %shard_map.84.refs_3_), channel_id=1, source_target_pairs={{0,3},{1,2},{2,1},{3,0},{4,7},{5,6},{6,5},{7,4},{8,11},{9,10},{10,... | collective-permute-start | bytes 1179656 | tf_op jit(solution)/shard_map/ppermute | solution.py:348
  (34 other events, 345.6 us)
